TPU v7x, 256 devices: a whole 4x4x8 slice. The times are simulated.
256 devices in a mesh: scan: 4 (over y), slab: 64 (over z, x, core).
Axes of the slice: x: 4, y: 4, z: 8, core: 2. Of those that a mesh axis runs over, the one named last changes fastest.
Arguments:
- volume: float32 [4, 32768, 1024], P('scan', 'slab'), may hold values from -108 to 108
- velocity0: float32 [4, 32768], P('scan', 'slab'), may hold values from -0.5 to 0.5
- fetch_slab: int32 [4, 2, 32768, 1], P('scan', None, 'slab'), may hold values from 0 to 63; in each aligned block of 512 rows (0 to 511, 512 to 1023, ..., all dimensions but the last counted through in order) at most 12 rows name the same one
- fetch_row: int32 [4, 2, 32768], P('scan', None, 'slab'), may hold values from 0 to 511
- modulus_class: int32 [4, 32768], P('scan', 'slab'), may hold values from 0 to 3
- modulus_table: float32 [4], replicated, may hold values from 200 to 3000
Outputs:
- velocity: float32 [4, 32768], P('scan', 'slab')
- misfit: float32 [4, 32768, 1024], P('scan', 'slab')
Inputs may be any that keep to these rules, and one draw needn't show every extreme that they name: `fetch_slab`: among the rows of one device for one direction, at most 12 name the same slab, a bound that some block reaches of them.
All inputs are finite; a program needn't handle non-finite values.
Results may differ from a plain program's by a relative error of at most 0.00011.
Values sent between devices are 32-bit elements; how exact they have to be, the bound alone decides.
A program may use at most 64 MiB of HBM per device.

v0:
```python
import math

import jax
import jax.numpy as jnp
from jax import lax
from jax.sharding import PartitionSpec as P

Y = 1024
BAND = 32
ITERS = 2


root_three = math.sqrt(3.0)
pole_value = math.sqrt(3.0) - 2.0


def with_halo(cells, sides, width):
    for axis, dim in sides:
        count = lax.axis_size(axis)
        ends = count - 1
        head = lax.slice_in_dim(cells, 0, width, axis=dim)
        tail = lax.slice_in_dim(cells, cells.shape[dim] - width, cells.shape[dim], axis=dim)
        cells = jnp.concatenate(
            [
                lax.ppermute(tail, axis, [(i, (i + 1) % count) for i in range(ends)]),
                cells,
                lax.ppermute(head, axis, [((i + 1) % count, i) for i in range(ends)]),
            ],
            axis=dim,
        )
    return cells


def passed_along(block, axis, distance):
    devices = range(lax.axis_size(axis))
    route = [(i - distance, i) for i in devices if i - distance in devices]
    return lax.ppermute(block, axis, route)


def filter_block(block_width, band_reach):
    offsets = (
        lax.broadcasted_iota(jnp.int32, (3 * block_width, block_width), 0)
        - block_width
        - lax.broadcasted_iota(jnp.int32, (3 * block_width, block_width), 1)
    )
    distance = jnp.abs(offsets)
    parity = 1.0 - 2.0 * (distance % 2).astype(jnp.float32)
    magnitude = jnp.exp(distance.astype(jnp.float32) * math.log(-pole_value))
    return jnp.where(
        distance <= band_reach, root_three * parity * magnitude, jnp.zeros_like(magnitude)
    )


def prefilter(voxels):
    length = voxels.shape[1]
    block_width = min(128, length)
    matrix = filter_block(block_width, BAND)
    padded = jnp.pad(voxels, ((0, 0), (block_width, block_width)))
    pieces = []
    for number in range(length // block_width):
        window = padded[:, number * block_width : number * block_width + 3 * block_width]
        pieces.append(
            jnp.dot(
                window, matrix, preferred_element_type=jnp.float32, precision=lax.Precision.HIGHEST
            )
        )
    return jnp.concatenate(pieces, axis=1)


def taylor_terms(coeffs):
    padded = jnp.pad(coeffs, ((0, 0), (1, 1)))
    before = padded[:, :-2]
    after = padded[:, 2:]
    value = (before + 4.0 * coeffs + after) / 6.0
    slope = 0.5 * (after - before)
    bend = after - 2.0 * coeffs + before
    return (value, slope, bend)


def residuals(forward, backward, voxels, velocity):
    moved = velocity[:, None]
    fwd_value, fwd_slope, fwd_bend = taylor_terms(forward)
    bwd_value, bwd_slope, bwd_bend = taylor_terms(backward)
    res_fwd = fwd_value + moved * fwd_slope + 0.5 * moved * moved * fwd_bend - voxels
    jac_fwd = fwd_slope + moved * fwd_bend
    res_bwd = bwd_value - moved * bwd_slope + 0.5 * moved * moved * bwd_bend - voxels
    jac_bwd = moved * bwd_bend - bwd_slope
    return (res_fwd, jac_fwd, res_bwd, jac_bwd)


def row_terms(forward, backward, voxels, velocity):
    res_fwd, jac_fwd, res_bwd, jac_bwd = residuals(forward, backward, voxels, velocity)
    linear = jnp.sum(jac_fwd * res_fwd + jac_bwd * res_bwd, axis=1)
    curvature = jnp.sum(jac_fwd * jac_fwd + jac_bwd * jac_bwd, axis=1)
    return (linear, curvature)


def plane_stencil(field):
    count_rows = field.shape[0]
    hops = Y // count_rows
    rimmed = with_halo(field[None, :], (("slab", 1),), 1)[0]
    lower = passed_along(field, "slab", hops)
    upper = passed_along(field, "slab", -hops)
    return 4.0 * field - rimmed[:-2] - rimmed[2:] - lower - upper


def on_device(volume, velocity0, fetch_slab, fetch_row, modulus_class, modulus_table):
    own_scan = volume[0]
    count_rows = own_scan.shape[0]
    devices = lax.axis_size("slab")
    capacity = max(2, 3 * count_rows // (2 * devices))
    ahead_rows = passed_along(own_scan, "scan", -1)
    behind = passed_along(own_scan, "scan", 1)
    peer_ids = fetch_slab[0, :, :, 0]
    wanted_rows = fetch_row[0]
    one_hot = (peer_ids[:, :, None] == lax.broadcasted_iota(jnp.int32, (1, 1, devices), 2)).astype(
        jnp.int32
    )
    running = jnp.cumsum(one_hot, axis=1) - one_hot
    slot_ids = jnp.sum(running * one_hot, axis=2)
    direction_ids = lax.broadcasted_iota(jnp.int32, (2, count_rows), 0)
    request_table = (
        jnp.zeros((2, devices, capacity), jnp.int32)
        .at[direction_ids, peer_ids, slot_ids]
        .set(wanted_rows)
    )
    asked_rows = lax.all_to_all(request_table, "slab", split_axis=1, concat_axis=1, tiled=True)
    forward_rows = jnp.take(ahead_rows, asked_rows[0], axis=0)
    backward_rows = jnp.take(behind, asked_rows[1], axis=0)
    arrived = lax.all_to_all(
        jnp.stack([forward_rows, backward_rows]), "slab", split_axis=1, concat_axis=1, tiled=True
    )
    fetched = arrived[direction_ids, peer_ids, slot_ids]
    filtered = prefilter(fetched.reshape(2 * count_rows, fetched.shape[2]))
    forward = filtered[:count_rows]
    backward = filtered[count_rows:]
    classes = lax.broadcasted_iota(jnp.int32, (1, modulus_table.shape[0]), 1)
    weight = jnp.sum(
        jnp.where(
            modulus_class[0][:, None] == classes,
            modulus_table[None, :],
            jnp.zeros_like(modulus_table)[None, :],
        ),
        axis=1,
    )
    stiffness = jnp.sqrt(weight)
    velocity = velocity0[0]
    for iteration in range(ITERS):
        linear, curvature = row_terms(forward, backward, own_scan, velocity)
        gradient = linear + stiffness * plane_stencil(stiffness * velocity)
        diagonal = curvature + 4.0 * stiffness * stiffness
        direction = gradient / diagonal
        scaled_dir = stiffness * direction
        bend_term = scaled_dir * plane_stencil(scaled_dir)
        totals = lax.psum(
            (jnp.sum(direction * gradient), jnp.sum(curvature * direction * direction + bend_term)),
            ("scan", "slab"),
        )
        velocity = velocity - totals[0] / totals[1] * direction
    res_fwd, jac_fwd, res_bwd, jac_bwd = residuals(forward, backward, own_scan, velocity)
    return (velocity[None, :], (res_fwd + res_bwd)[None])


def solution(mesh):
    return jax.shard_map(
        on_device,
        mesh=mesh,
        in_specs=(
            P("scan", "slab", None),
            P("scan", "slab"),
            P("scan", None, "slab", None),
            P("scan", None, "slab"),
            P("scan", "slab"),
            P(),
        ),
        out_specs=(P("scan", "slab"), P("scan", "slab", None)),
        check_vma=False,
    )
```

profile of v0, /device:TPU:1, one launch (start us, length us, event | category | flops | bytes accessed | tf_op | source)
XLA Modules:
  0.0 537.0 jit_solution(10035754950157322251)
XLA Ops:
  4.9 6.0 %collective-permute-start.1 = (f32[512,1024]{0,1:T(8,128)}, f32[512,1024]{0,1:T(8,128)}, u32[]{:S(2)}, u32[]{:S(2)}) collective-permute-start(f32[512,1024]{0,1:T(8,128)} %bitcast.6), channel_id=1, source_target_pairs={{0,64},{64,128},{128,192},{1,65},{65,129},{129,193},{2,66},{66,130... | collective-permute-start | bytes 6291464 | tf_op jit(solution)/shard_map/ppermute | solution.py:37
  14.2 4.3 scatter_custom_fusion
  18.7 23.1 %all_to_all.10 = s32[2,64,12]{2,0,1:T(2,128)S(1)} all-to-all(s32[2,64,12]{2,0,1:T(2,128)S(1)} %copy.60), channel_id=1, replica_groups=mesh['scan'=4,'slab'=64] {'slab'}, dimensions={1} | all-to-all | bytes 12288 | tf_op jit(solution)/shard_map/all_to_all | solution.py:127
  42.7 8.4 %collective-permute-done = f32[512,1024]{0,1:T(8,128)} collective-permute-done((f32[512,1024]{0,1:T(8,128)}, f32[512,1024]{0,1:T(8,128)}, u32[]{:S(2)}, u32[]{:S(2)}) %collective-permute-start) | collective-permute-done | bytes 2097184 | tf_op jit(solution)/shard_map/ppermute | solution.py:37
  56.6 4.6 reshape.161
  63.1 3.7 gather_fusion.2
  66.8 4.6 reshape.165
  71.4 3.8 select_bitcast_fusion
  75.3 4.2 pad_maximum_fusion
  79.5 12.0 %copy.70 = f32[2,64,12,1024]{3,0,2,1:T(2,128)} copy(f32[2,64,12,1024]{3,2,1,0:T(8,128)} %pad_maximum_fusion) | data formatting | bytes 12582912 | tf_op jit(solution)/shard_map/stack | solution.py:131
  91.4 15.3 %all-to-all-start.1 = ((f32[2,64,12,1024]{3,0,2,1:T(2,128)}), f32[2,64,12,1024]{3,0,2,1:T(2,128)}, u32[]{:S(2)}, u32[]{:S(2)}) async-start(f32[2,64,12,1024]{3,0,2,1:T(2,128)} %copy.70), calls=%async_computation.1 | async-start | bytes 12582912 | tf_op jit(solution)/shard_map/all_to_all | solution.py:130
  112.0 4.8 collective-permute-start.2
  116.9 13.8 %collective-permute-start.3 = (f32[1,1]{1,0:T(1,128)}, f32[1,1]{1,0:T(1,128)}, u32[]{:S(2)}, u32[]{:S(2)}) collective-permute-start(f32[1,1]{1,0:T(1,128)} %get-tuple-element.67), channel_id=1, source_target_pairs={{1,0},{2,1},{3,2},{4,3},{5,4},{6,5},{7,6},{8,7},{9,8},{10,9},{11,1... | collective-permute-start | bytes 20 | tf_op jit(solution)/shard_map/ppermute | solution.py:27
  132.1 113.6 %all-to-all-done.1 = f32[2,64,12,1024]{3,0,2,1:T(2,128)} async-done(((f32[2,64,12,1024]{3,0,2,1:T(2,128)}), f32[2,64,12,1024]{3,0,2,1:T(2,128)}, u32[]{:S(2)}, u32[]{:S(2)}) %all-to-all-start.1) | async-done | bytes 6291488 | tf_op jit(solution)/shard_map/all_to_all | solution.py:130
  245.6 9.1 %copy.71 = f32[2,64,12,1024]{3,1,2,0:T(8,128)} copy(f32[2,64,12,1024]{3,0,2,1:T(2,128)} %all-to-all-done.1) | data formatting | bytes 12582912 | tf_op jit(solution)/shard_map/all_to_all | solution.py:130
  254.7 21.5 %gather_fusion = f32[1024,1024]{1,0:T(8,128)} fusion(f32[2,64,12,1024]{3,1,2,0:T(8,128)} %copy.71, s32[1024]{0:T(1024)S(1)} %bitcast.67), kind=kCustom, calls=%fused_computation.2 | custom fusion | bytes 8400896 | tf_op jit(solution)/shard_map/gather | solution.py:133
  293.9 7.1 %add_reduce_fusion.2 = (f32[512]{0:T(512)S(1)}, f32[512]{0:T(512)S(1)}, f32[512,1024]{0,1:T(8,128)S(1)}, f32[512,1024]{0,1:T(8,128)}, f32[512,1024]{0,1:T(8,128)...) fusion(f32[512]{0:T(512)S(1)} %bitcast.69, f32[1,512,1024]{1,2,0:T(8,128)} %copy.63, ...), kind=kLoop, calls=%fused_computation.14 | loop fusion | flops 20970496 | bytes 18884608 | tf_op jit(solution)/shard_map/reduce_sum | solution.py:94
  306.0 7.2 %collective-permute-start.6 = (f32[1,1]{1,0:T(1,128)}, f32[1,1]{1,0:T(1,128)}, u32[]{:S(2)}, u32[]{:S(2)}) collective-permute-start(f32[1,1]{1,0:T(1,128)} %get-tuple-element.62), channel_id=1, source_target_pairs={{0,1},{1,2},{2,3},{3,4},{4,5},{5,6},{6,7},{7,8},{8,9},{9,10},{10,1... | collective-permute-start | bytes 20 | tf_op jit(solution)/shard_map/ppermute | solution.py:25
  320.4 78.0 %all-reduce.4 = (f32[]{:T(128)}, f32[]{:T(128)}) all-reduce(f32[]{:T(128)} %get-tuple-element.22, f32[]{:T(128)} %get-tuple-element.21), channel_id=1, replica_groups=mesh['scan'=4,'slab'=64] {'scan','slab'}, use_global_device_ids=true, to_apply=%region_8.10 | all-reduce | flops 2 | bytes 16 | tf_op jit(solution)/shard_map/psum | solution.py:155
  404.3 5.1 collective-permute-start.10
  411.3 5.5 %add_reduce_fusion = (f32[512]{0:T(512)S(1)}, f32[512]{0:T(512)S(1)}) fusion(f32[512,1024]{0,1:T(8,128)} %get-tuple-element.42, f32[512,1024]{0,1:T(8,128)} %get-tuple-element.41, f32[512,1024]{0,1:T(8,128)} %get-tuple-element.40, f32[512,1024]{0,1:T(8,128)} %get-tuple-element.39, f32[512]{0:T(512)S(1)} %get-tuple-element.33, ...), kind=kLoop, calls=%fused_computation.10 | loop fusion | flops 12581888 | bytes 14690304 | tf_op jit(solution)/shard_map/reduce_sum | solution.py:94
  422.4 5.9 %collective-permute-start.14 = (f32[1,1]{1,0:T(1,128)}, f32[1,1]{1,0:T(1,128)}, u32[]{:S(2)}, u32[]{:S(2)}) collective-permute-start(f32[1,1]{1,0:T(1,128)} %get-tuple-element.52), channel_id=1, source_target_pairs={{0,1},{1,2},{2,3},{3,4},{4,5},{5,6},{6,7},{7,8},{8,9},{9,10},{10,1... | collective-permute-start | bytes 20 | tf_op jit(solution)/shard_map/ppermute | solution.py:25
  435.5 89.2 %all-reduce.3 = (f32[]{:T(128)}, f32[]{:T(128)}) all-reduce(f32[]{:T(128)} %get-tuple-element.20, f32[]{:T(128)} %get-tuple-element.19), channel_id=1, replica_groups=mesh['scan'=4,'slab'=64] {'scan','slab'}, use_global_device_ids=true, to_apply=%region_14.16 | all-reduce | flops 2 | bytes 16 | tf_op jit(solution)/shard_map/psum | solution.py:155
  526.1 7.8 %add_bitcast_fusion = f32[1,512,1024]{1,2,0:T(8,128)} fusion(f32[512,1024]{0,1:T(8,128)} %get-tuple-element.41, f32[512,1024]{0,1:T(8,128)} %get-tuple-element.38, f32[512,1024]{0,1:T(8,128)} %get-tuple-element.42, f32[512,1024]{0,1:T(8,128)} %get-tuple-element.40, f32[512,1024]{0,1:T(8,128)S(1)} %get-tuple-element.37, f32[512,1024]{0,1:T(8,128)} %get-tuple-element.39, ...), kind=kLoop, calls=%fused_computation.9 | loop fusion | flops 5767168 | bytes 16781312 | tf_op jit(solution)/shard_map/broadcast_in_dim | solution.py:161
  (112 shorter events, 74.3 us)
Async XLA Ops:
  0.6 13.4 %copy-start.8 = (s32[3]{0:T(128)S(1)}, s32[3]{0:T(128)}, u32[]{:S(2)}) copy-start(s32[3]{0:T(128)} %constant.82) | copy-start | bytes 40
  0.7 13.5 %copy-start.4 = (s32[1,2,512]{2,1,0:T(2,128)S(1)}, s32[1,2,512]{2,1,0:T(2,128)}, u32[]{:S(2)}) copy-start(s32[1,2,512]{2,1,0:T(2,128)} %param.11) | copy-start | bytes 12292
  3.6 47.5 %collective-permute-start = (f32[512,1024]{0,1:T(8,128)}, f32[512,1024]{0,1:T(8,128)}, u32[]{:S(2)}, u32[]{:S(2)}) collective-permute-start(f32[512,1024]{0,1:T(8,128)} %bitcast.6), channel_id=1, source_target_pairs={{64,0},{128,64},{192,128},{65,1},{129,65},{193,129},{66,2},{130,66... | collective-permute-start | bytes 6291464 | tf_op jit(solution)/shard_map/ppermute | solution.py:37
  4.9 56.4 %collective-permute-start.1 = (f32[512,1024]{0,1:T(8,128)}, f32[512,1024]{0,1:T(8,128)}, u32[]{:S(2)}, u32[]{:S(2)}) collective-permute-start(f32[512,1024]{0,1:T(8,128)} %bitcast.6), channel_id=1, source_target_pairs={{0,64},{64,128},{128,192},{1,65},{65,129},{129,193},{2,66},{66,130... | collective-permute-start | bytes 6291464 | tf_op jit(solution)/shard_map/ppermute | solution.py:37
  91.4 15.3 %copy-start.5 = (s32[1,512]{1,0:T(1,128)S(1)}, s32[1,512]{1,0:T(1,128)}, u32[]{:S(2)}) copy-start(s32[1,512]{1,0:T(1,128)} %param.12) | copy-start | bytes 6148
  91.4 15.4 %copy-start.6 = (f32[4]{0:T(128)S(1)}, f32[4]{0:T(128)}, u32[]{:S(2)}) copy-start(f32[4]{0:T(128)} %param.13) | copy-start | bytes 52
  91.4 15.4 %copy-start.1 = (f32[1,512]{1,0:T(1,128)S(1)}, f32[1,512]{1,0:T(1,128)}, u32[]{:S(2)}) copy-start(f32[1,512]{1,0:T(1,128)} %param.9) | copy-start | bytes 6148
  91.4 154.2 %all-to-all-start.1 = ((f32[2,64,12,1024]{3,0,2,1:T(2,128)}), f32[2,64,12,1024]{3,0,2,1:T(2,128)}, u32[]{:S(2)}, u32[]{:S(2)}) async-start(f32[2,64,12,1024]{3,0,2,1:T(2,128)} %copy.70), calls=%async_computation.1 | async-start | bytes 12582912 | tf_op jit(solution)/shard_map/all_to_all | solution.py:130
  106.9 194.1 %collective-permute-start.4 = (f32[512]{0:T(512)S(1)}, f32[512]{0:T(512)S(1)}, u32[]{:S(2)}, u32[]{:S(2)}) collective-permute-start(f32[512]{0:T(512)S(1)} %get-tuple-element.69), channel_id=1, source_target_pairs={{0,2},{1,3},{2,4},{3,5},{4,6},{5,7},{6,8},{7,9},{8,10},{9,11},{10,... | collective-permute-start | bytes 6152 | tf_op jit(solution)/shard_map/ppermute | solution.py:37
  110.1 190.8 %collective-permute-start.5 = (f32[512]{0:T(512)S(1)}, f32[512]{0:T(512)S(1)}, u32[]{:S(2)}, u32[]{:S(2)}) collective-permute-start(f32[512]{0:T(512)S(1)} %get-tuple-element.69), channel_id=1, source_target_pairs={{2,0},{3,1},{4,2},{5,3},{6,4},{7,5},{8,6},{9,7},{10,8},{11,9},{12,... | collective-permute-start | bytes 6152 | tf_op jit(solution)/shard_map/ppermute | solution.py:37
  112.0 18.7 %collective-permute-start.2 = (f32[1,1]{1,0:T(1,128)}, f32[1,1]{1,0:T(1,128)}, u32[]{:S(2)}, u32[]{:S(2)}) collective-permute-start(f32[1,1]{1,0:T(1,128)} %get-tuple-element.66), channel_id=1, source_target_pairs={{0,1},{1,2},{2,3},{3,4},{4,5},{5,6},{6,7},{7,8},{8,9},{9,10},{10,1... | collective-permute-start | bytes 20 | tf_op jit(solution)/shard_map/ppermute | solution.py:25
  116.9 13.9 %collective-permute-start.3 = (f32[1,1]{1,0:T(1,128)}, f32[1,1]{1,0:T(1,128)}, u32[]{:S(2)}, u32[]{:S(2)}) collective-permute-start(f32[1,1]{1,0:T(1,128)} %get-tuple-element.67), channel_id=1, source_target_pairs={{1,0},{2,1},{3,2},{4,3},{5,4},{6,5},{7,6},{8,7},{9,8},{10,9},{11,1... | collective-permute-start | bytes 20 | tf_op jit(solution)/shard_map/ppermute | solution.py:27
  301.0 18.8 %collective-permute-start.8 = (f32[512]{0:T(512)S(1)}, f32[512]{0:T(512)S(1)}, u32[]{:S(2)}, u32[]{:S(2)}) collective-permute-start(f32[512]{0:T(512)S(1)} %get-tuple-element.34), channel_id=1, source_target_pairs={{0,2},{1,3},{2,4},{3,5},{4,6},{5,7},{6,8},{7,9},{8,10},{9,11},{10,... | collective-permute-start | bytes 6152 | tf_op jit(solution)/shard_map/ppermute | solution.py:37
  304.2 15.6 %collective-permute-start.9 = (f32[512]{0:T(512)S(1)}, f32[512]{0:T(512)S(1)}, u32[]{:S(2)}, u32[]{:S(2)}) collective-permute-start(f32[512]{0:T(512)S(1)} %get-tuple-element.34), channel_id=1, source_target_pairs={{2,0},{3,1},{4,2},{5,3},{6,4},{7,5},{8,6},{9,7},{10,8},{11,9},{12,... | collective-permute-start | bytes 6152 | tf_op jit(solution)/shard_map/ppermute | solution.py:37
  306.0 9.1 %collective-permute-start.6 = (f32[1,1]{1,0:T(1,128)}, f32[1,1]{1,0:T(1,128)}, u32[]{:S(2)}, u32[]{:S(2)}) collective-permute-start(f32[1,1]{1,0:T(1,128)} %get-tuple-element.62), channel_id=1, source_target_pairs={{0,1},{1,2},{2,3},{3,4},{4,5},{5,6},{6,7},{7,8},{8,9},{9,10},{10,1... | collective-permute-start | bytes 20 | tf_op jit(solution)/shard_map/ppermute | solution.py:25
  313.2 5.2 collective-permute-start.7
  399.8 18.4 %collective-permute-start.12 = (f32[512]{0:T(512)S(1)}, f32[512]{0:T(512)S(1)}, u32[]{:S(2)}, u32[]{:S(2)}) collective-permute-start(f32[512]{0:T(512)S(1)} %get-tuple-element.32), channel_id=1, source_target_pairs={{0,2},{1,3},{2,4},{3,5},{4,6},{5,7},{6,8},{7,9},{8,10},{9,11},{10,... | collective-permute-start | bytes 6152 | tf_op jit(solution)/shard_map/ppermute | solution.py:37
  402.4 15.8 %collective-permute-start.13 = (f32[512]{0:T(512)S(1)}, f32[512]{0:T(512)S(1)}, u32[]{:S(2)}, u32[]{:S(2)}) collective-permute-start(f32[512]{0:T(512)S(1)} %get-tuple-element.32), channel_id=1, source_target_pairs={{2,0},{3,1},{4,2},{5,3},{6,4},{7,5},{8,6},{9,7},{10,8},{11,9},{12,... | collective-permute-start | bytes 6152 | tf_op jit(solution)/shard_map/ppermute | solution.py:37
  404.3 12.6 %collective-permute-start.10 = (f32[1,1]{1,0:T(1,128)}, f32[1,1]{1,0:T(1,128)}, u32[]{:S(2)}, u32[]{:S(2)}) collective-permute-start(f32[1,1]{1,0:T(1,128)} %get-tuple-element.56), channel_id=1, source_target_pairs={{0,1},{1,2},{2,3},{3,4},{4,5},{5,6},{6,7},{7,8},{8,9},{9,10},{10,1... | collective-permute-start | bytes 20 | tf_op jit(solution)/shard_map/ppermute | solution.py:25
  409.4 7.5 %collective-permute-start.11 = (f32[1,1]{1,0:T(1,128)}, f32[1,1]{1,0:T(1,128)}, u32[]{:S(2)}, u32[]{:S(2)}) collective-permute-start(f32[1,1]{1,0:T(1,128)} %get-tuple-element.57), channel_id=1, source_target_pairs={{1,0},{2,1},{3,2},{4,3},{5,4},{6,5},{7,6},{8,7},{9,8},{10,9},{11,1... | collective-permute-start | bytes 20 | tf_op jit(solution)/shard_map/ppermute | solution.py:27
  418.3 16.6 %collective-permute-start.16 = (f32[512]{0:T(512)S(1)}, f32[512]{0:T(512)S(1)}, u32[]{:S(2)}, u32[]{:S(2)}) collective-permute-start(f32[512]{0:T(512)S(1)} %get-tuple-element.29), channel_id=1, source_target_pairs={{0,2},{1,3},{2,4},{3,5},{4,6},{5,7},{6,8},{7,9},{8,10},{9,11},{10,... | collective-permute-start | bytes 6152 | tf_op jit(solution)/shard_map/ppermute | solution.py:37
  420.5 14.4 %collective-permute-start.17 = (f32[512]{0:T(512)S(1)}, f32[512]{0:T(512)S(1)}, u32[]{:S(2)}, u32[]{:S(2)}) collective-permute-start(f32[512]{0:T(512)S(1)} %get-tuple-element.29), channel_id=1, source_target_pairs={{2,0},{3,1},{4,2},{5,3},{6,4},{7,5},{8,6},{9,7},{10,8},{11,9},{12,... | collective-permute-start | bytes 6152 | tf_op jit(solution)/shard_map/ppermute | solution.py:37
  422.4 7.9 %collective-permute-start.14 = (f32[1,1]{1,0:T(1,128)}, f32[1,1]{1,0:T(1,128)}, u32[]{:S(2)}, u32[]{:S(2)}) collective-permute-start(f32[1,1]{1,0:T(1,128)} %get-tuple-element.52), channel_id=1, source_target_pairs={{0,1},{1,2},{2,3},{3,4},{4,5},{5,6},{6,7},{7,8},{8,9},{9,10},{10,1... | collective-permute-start | bytes 20 | tf_op jit(solution)/shard_map/ppermute | solution.py:25
  428.3 5.2 collective-permute-start.15
  (4 other events, 34.7 us)
where the time goes:
time: 541 us; the launch traced here: 537 us
  blocking collectives  190 us (35%)
  waiting for transfers between devices  128 us (24%)
  starting transfers between devices  81.7 us (15%)
  local copies, waits for them, and re-layouts  77.3 us (14%)
  other arithmetic  38.1 us (7%)
  matrix products  17 us (3%)
    psum x2, blocking collectives, on_device(): lax.psum((jnp.sum(direction * gradient), jnp.sum(curvature * direction *...  167 us
    all_to_all x1, waiting for transfers between devices, on_device(): lax.all_to_all(jnp.stack([forward_rows, backward_rows]), 'slab', split_ax...  114 us
    ppermute x10, starting transfers between devices, passed_along(): return lax.ppermute(block, axis, route)  23.7 us
    all_to_all x1, blocking collectives, on_device(): lax.all_to_all(request_table, 'slab', split_axis=1, concat_axis=1, tiled=...  23.1 us
    ppermute x4, starting transfers between devices, with_halo(): lax.ppermute(tail, axis, [(i, (i + 1) % count) for i in range(ends)])  23 us
    gather x1, local copies, waits for them, and re-layouts, on_device(): fetched = arrived[direction_ids, peer_ids, slot_ids]  21.5 us
    ppermute x4, starting transfers between devices, with_halo(): lax.ppermute(head, axis, [((i + 1) % count, i) for i in range(ends)])  19.6 us
    dot_general x8, matrix products, prefilter(): jnp.dot(window, matrix, preferred_element_type=jnp.float32, precision=lax...  17 us
  transfers between devices with their start and end apart: 19, of which 4 were waited for; matrix products, arithmetic and copies ran while one was open for 16% of the time, Pallas kernels for 0%

commit v1 on v0

v1 whole, which is shorter than its diff:
```python
import math

import jax
import jax.numpy as jnp
import numpy as np
from jax import lax
from jax.experimental import pallas as pl
from jax.experimental.pallas import tpu as pltpu
from jax.sharding import PartitionSpec as P

BAND = 32
ITERS = 2
CAP = 12
LANES = 128
MESH = pl.DeviceIdType.MESH

root_three = math.sqrt(3.0)
pole_value = math.sqrt(3.0) - 2.0


def slots_kernel(peer_ref, row_ref, request_ref, place_ref):
    slabs = request_ref.shape[1]
    rows = peer_ref.shape[1]
    earlier = (
        lax.broadcasted_iota(jnp.int32, (rows, rows), 0)
        < lax.broadcasted_iota(jnp.int32, (rows, rows), 1)
    ).astype(jnp.float32).astype(jnp.bfloat16)
    for side in range(2):
        peer = peer_ref[side : side + 1, :]
        row = row_ref[side : side + 1, :]
        named = (lax.broadcasted_iota(jnp.int32, (slabs, rows), 0) == peer).astype(jnp.float32)
        named16 = named.astype(jnp.bfloat16)
        before = jnp.dot(named16, earlier, preferred_element_type=jnp.float32)
        slot = jnp.sum(before * named, axis=0, keepdims=True).astype(jnp.int32)
        at_slot = (lax.broadcasted_iota(jnp.int32, (LANES, rows), 0) == slot).astype(jnp.float32)
        high = (row // 16).astype(jnp.float32)
        low = (row % 16).astype(jnp.float32)
        contract = (((1,), (1,)), ((), ()))
        high_part = lax.dot_general(
            named16, (at_slot * high).astype(jnp.bfloat16), contract,
            preferred_element_type=jnp.float32,
        )
        low_part = lax.dot_general(
            named16, (at_slot * low).astype(jnp.bfloat16), contract,
            preferred_element_type=jnp.float32,
        )
        request_ref[side] = (16.0 * high_part + low_part).astype(jnp.int32)
        place_ref[side : side + 1, :] = side * slabs * CAP + peer * CAP + slot


def displaced(slab, number):
    phase = number % 8
    wave = number // 8
    shift_z = jnp.where(phase % 2 == 0, (8 - phase // 2) % 8, (phase + 1) // 2)
    shift_x = 2 * (wave % 2) + wave // 4
    shift_c = (wave // 2) % 2
    core = (slab % 2 + shift_c) % 2
    at_x = ((slab // 2) % 4 + shift_x) % 4
    at_z = (slab // 8 + shift_z) % 8
    return (at_z * 4 + at_x) * 2 + core


def exchange_kernel(
    request_ref, volume_ref, arrived_ref,
    asked, asked_scalar, by_row, packed, relay,
    ask_send, ask_recv, local_sem, row_send, row_recv, relay_recv, relay_send,
):
    scan = lax.axis_index("scan")
    slab = lax.axis_index("slab")
    slabs = request_ref.shape[1]
    rows = volume_ref.shape[0]
    last = 3
    edge = jnp.logical_or(scan == 0, scan == last)
    inner_down = scan >= 1
    inner_up = scan <= last - 1

    barrier = pltpu.get_barrier_semaphore()

    def greet(number, carry):
        @pl.when(inner_down)
        def _():
            pl.semaphore_signal(barrier, inc=1, device_id=(scan - 1, number), device_id_type=MESH)

        @pl.when(inner_up)
        def _():
            pl.semaphore_signal(barrier, inc=1, device_id=(scan + 1, number), device_id_type=MESH)

        @pl.when(jnp.logical_and(edge, number != slab))
        def _():
            pl.semaphore_signal(barrier, inc=1, device_id=(scan, number), device_id_type=MESH)

        return carry

    lax.fori_loop(0, slabs, greet, 0)

    def relayout(block, carry):
        base = pl.multiple_of(block * 8, 8)
        for part in range(8):
            by_row[pl.ds(base, 8), part, :] = volume_ref[
                pl.ds(base, 8), part * LANES : (part + 1) * LANES
            ]
        return carry

    lax.fori_loop(0, rows // 8, relayout, 0)
    pl.semaphore_wait(barrier, jnp.where(edge, 2 * slabs - 1, 2 * slabs))

    def ask_copy(side, number):
        return pltpu.make_async_remote_copy(
            src_ref=request_ref.at[side, number],
            dst_ref=asked.at[side, slab],
            send_sem=ask_send.at[side],
            recv_sem=ask_recv.at[side],
            device_id=(scan + 1 - 2 * side, number),
            device_id_type=MESH,
        )

    def ask(number, carry):
        target = displaced(slab, number)

        @pl.when(inner_up)
        def _():
            ask_copy(0, target).start()

        @pl.when(inner_down)
        def _():
            ask_copy(1, target).start()

        return carry

    lax.fori_loop(0, slabs, ask, 0)

    def whole_ask(side):
        return pltpu.make_async_remote_copy(
            src_ref=request_ref.at[side],
            dst_ref=asked.at[side],
            send_sem=ask_send.at[side],
            recv_sem=ask_recv.at[side],
            device_id=(scan, slab),
            device_id_type=MESH,
        )

    def take_asked(side):
        whole_ask(side).wait_recv()
        copy = pltpu.make_async_copy(asked.at[side], asked_scalar.at[side], local_sem)
        copy.start()
        copy.wait()

    @pl.when(inner_down)
    def _():
        take_asked(0)

    @pl.when(inner_up)
    def _():
        take_asked(1)

    def pack(side, number, target):
        for slot in range(CAP):
            row = asked_scalar[side, target, 0, slot]
            packed[side, number, slot] = by_row[row]

    def row_copy(source, side, target, target_scan, send_sem):
        return pltpu.make_async_remote_copy(
            src_ref=source,
            dst_ref=arrived_ref.at[side, slab],
            send_sem=send_sem,
            recv_sem=row_recv.at[side],
            device_id=(target_scan, target),
            device_id_type=MESH,
        )

    def relay_copy(side, number, relay_number, target_scan):
        return pltpu.make_async_remote_copy(
            src_ref=packed.at[side, number],
            dst_ref=relay.at[relay_number],
            send_sem=row_send.at[side],
            recv_sem=relay_recv.at[relay_number],
            device_id=(target_scan, slab),
            device_id_type=MESH,
        )

    def serve(side, number, target, relayed_scan):
        target_scan = scan - 1 + 2 * side
        relay_number = (number // 16) * 8 + number % 8
        relayed = jnp.logical_and(scan == relayed_scan, (number // 8) % 2 == 1)
        pack(side, number, target)

        @pl.when(relayed)
        def _():
            relay_copy(side, number, relay_number, target_scan).start()

        @pl.when(jnp.logical_not(relayed))
        def _():
            row_copy(packed.at[side, number], side, target, target_scan, row_send.at[side]).start()

    def send(number, carry):
        target = displaced(slab, number)

        @pl.when(inner_down)
        def _():
            serve(0, number, target, 1)

        @pl.when(inner_up)
        def _():
            serve(1, number, target, 2)

        return carry

    lax.fori_loop(0, slabs, send, 0)

    def pass_on(side):
        def forward(relay_number, carry):
            number = (relay_number // 8) * 16 + 8 + relay_number % 8
            pltpu.make_async_remote_copy(
                src_ref=relay.at[relay_number],
                dst_ref=relay.at[relay_number],
                send_sem=relay_send,
                recv_sem=relay_recv.at[relay_number],
                device_id=(scan, slab),
                device_id_type=MESH,
            ).wait_recv()
            row_copy(
                relay.at[relay_number], side, displaced(slab, number), scan, relay_send
            ).start()
            return carry

        lax.fori_loop(0, slabs // 2, forward, 0)

    @pl.when(scan == 0)
    def _():
        pass_on(0)

    @pl.when(scan == last)
    def _():
        pass_on(1)

    def whole_rows(side):
        return pltpu.make_async_remote_copy(
            src_ref=packed.at[side],
            dst_ref=arrived_ref.at[side],
            send_sem=row_send.at[side],
            recv_sem=row_recv.at[side],
            device_id=(scan, slab),
            device_id_type=MESH,
        )

    @pl.when(inner_up)
    def _():
        whole_ask(0).wait_send()
        whole_rows(1).wait_send()
        whole_rows(0).wait_recv()

    @pl.when(inner_down)
    def _():
        whole_ask(1).wait_send()
        whole_rows(0).wait_send()
        whole_rows(1).wait_recv()

    @pl.when(edge)
    def _():
        pltpu.make_async_remote_copy(
            src_ref=relay,
            dst_ref=relay,
            send_sem=relay_send,
            recv_sem=relay_recv.at[0],
            device_id=(scan, slab),
            device_id_type=MESH,
        ).wait_send()


def filter_parts():
    source = np.arange(LANES)[:, None]
    column = np.arange(2 * LANES)[None, :]
    lane = column % LANES
    beside = np.where(lane < LANES // 2, lane + LANES, lane - LANES)
    distance = np.abs(source - np.where(column < LANES, lane, beside))
    matrix = np.where(distance <= BAND, root_three * pole_value ** distance, 0.0)
    matrix = matrix.astype(np.float32)
    high = matrix.astype(jnp.bfloat16)
    low = (matrix - high.astype(np.float32)).astype(jnp.bfloat16)
    return jnp.asarray(high), jnp.asarray(low)


def terms_kernel(
    place_ref, arrived_ref, volume_ref, high_ref, low_ref,
    moment_ref, part0_ref, part1_ref, part2_ref, gathered, middle, beside, partial,
):
    rows = volume_ref.shape[0]
    parts = volume_ref.shape[1] // LANES
    scan = lax.axis_index("scan")
    first_row = pl.program_id(0) * rows
    lane = lax.broadcasted_iota(jnp.int32, (8, LANES), 1)

    for side in range(2):
        def fetch(group, carry):
            for one in range(8):
                row = group * 8 + one
                place = place_ref[side, first_row + row]
                gathered[side, pl.ds(pl.multiple_of(row * 8, 8), 8), :] = arrived_ref[
                    pl.ds(pl.multiple_of(place * 8, 8), 8), :
                ]
            return carry

        lax.fori_loop(0, rows // 8, fetch, 0)
        present = (scan <= 2) if side == 0 else (scan >= 1)
        for part in range(parts):
            voxels = gathered[side, pl.ds(part, rows, stride=parts), :]
            voxels = jnp.where(present, voxels, 0.0)
            top = voxels.astype(jnp.bfloat16)
            rest = (voxels - top.astype(jnp.float32)).astype(jnp.bfloat16)
            both = (
                jnp.dot(top, high_ref[...], preferred_element_type=jnp.float32)
                + jnp.dot(rest, high_ref[...], preferred_element_type=jnp.float32)
                + jnp.dot(top, low_ref[...], preferred_element_type=jnp.float32)
            )
            middle[side, part] = both[:, :LANES]
            beside[side, part] = both[:, LANES:]

    zero = jnp.zeros((8, LANES), jnp.float32)

    def combine(group, carry):
        at = pl.ds(pl.multiple_of(group * 8, 8), 8)
        values, slopes, bends = [], [], []
        for side in range(2):
            coeffs = []
            for part in range(parts):
                left = beside[side, part - 1, at, :] if part > 0 else zero
                right = beside[side, part + 1, at, :] if part < parts - 1 else zero
                coeffs.append(middle[side, part, at, :] + jnp.where(lane < LANES // 2, left, right))
            to_right = [pltpu.roll(one, 1, 1) for one in coeffs]
            to_left = [pltpu.roll(one, LANES - 1, 1) for one in coeffs]
            value, slope, bend = [], [], []
            for part in range(parts):
                before = jnp.where(lane == 0, to_right[part - 1] if part > 0 else zero, to_right[part])
                after = jnp.where(
                    lane == LANES - 1, to_left[part + 1] if part < parts - 1 else zero, to_left[part]
                )
                ends = before + after
                value.append((ends + 4.0 * coeffs[part]) * (1.0 / 6.0))
                slope.append(0.5 * (after - before))
                bend.append(ends - 2.0 * coeffs[part])
            values.append(value)
            slopes.append(slope)
            bends.append(bend)
        sums = [zero] * 5
        for part in range(parts):
            columns = slice(part * LANES, (part + 1) * LANES)
            voxels = volume_ref[at, columns]
            off_f = values[0][part] - voxels
            off_b = values[1][part] - voxels
            slope_f, slope_b = slopes[0][part], slopes[1][part]
            bend_f, bend_b = bends[0][part], bends[1][part]
            sums[0] += slope_f * off_f - slope_b * off_b
            sums[1] += bend_f * off_f + bend_b * off_b
            sums[2] += slope_f * slope_f + slope_b * slope_b
            sums[3] += slope_f * bend_f - slope_b * bend_b
            sums[4] += bend_f * bend_f + bend_b * bend_b
            part0_ref[at, columns] = off_f + off_b
            part1_ref[at, columns] = slope_f - slope_b
            part2_ref[at, columns] = 0.5 * (bend_f + bend_b)
        for number in range(5):
            partial[number, at, :] = sums[number]
        return carry

    lax.fori_loop(0, rows // 8, combine, 0)
    ones = jnp.ones((8, LANES), jnp.float32)
    for number in range(5):
        total = lax.dot_general(
            ones, partial[number], (((1,), (1,)), ((), ())),
            preferred_element_type=jnp.float32, precision=lax.Precision.HIGHEST,
        )
        moment_ref[number : number + 1, :] = total[0:1, :]


def descent_kernel(
    table_ref, moment_ref, velocity_ref, class_ref, out_ref,
    fields, halos, totals, near_box, far_box,
    halo_send, halo_recv, near_send, near_recv, far_send, far_recv,
):
    scan = lax.axis_index("scan")
    slab = lax.axis_index("slab")
    rows = velocity_ref.shape[1]
    slabs = 64
    scans = 4
    layers = 8
    group = slabs // layers
    place = slab % group
    layer = slab // group
    fars = scans * layers
    own_far = scan * layers + layer
    steps = ((-1, slab >= 1), (1, slab <= slabs - 2), (-2, slab >= 2), (2, slab <= slabs - 3))

    def near_peer(number):
        return (scan, layer * group + (place + 1 + number) % group)

    def far_peer(number):
        other = (own_far + 1 + number) % fars
        return (other // layers, (other % layers) * group + place)

    barrier = pltpu.get_barrier_semaphore()
    expected = group - 1 + fars - 1
    for step, exists in steps:
        @pl.when(exists)
        def _():
            pl.semaphore_signal(barrier, inc=1, device_id=(scan, slab + step), device_id_type=MESH)

        expected = expected + jnp.where(exists, 1, 0)

    def greet_near(number, carry):
        pl.semaphore_signal(barrier, inc=1, device_id=near_peer(number), device_id_type=MESH)
        return carry

    def greet_far(number, carry):
        pl.semaphore_signal(barrier, inc=1, device_id=far_peer(number), device_id_type=MESH)
        return carry

    lax.fori_loop(0, group - 1, greet_near, 0)
    lax.fori_loop(0, fars - 1, greet_far, 0)

    weight = jnp.zeros((1, rows), jnp.float32)
    for number in range(4):
        weight = jnp.where(class_ref[...] == number, table_ref[number], weight)
    stiffness = jnp.sqrt(weight)
    velocity = velocity_ref[...]
    lane = lax.broadcasted_iota(jnp.int32, (1, rows), 1)
    pl.semaphore_wait(barrier, expected)

    def halo_copy(turn, number, step):
        return pltpu.make_async_remote_copy(
            src_ref=fields.at[turn],
            dst_ref=halos.at[turn, number],
            send_sem=halo_send.at[turn, number],
            recv_sem=halo_recv.at[turn, number],
            device_id=(scan, slab + step),
            device_id_type=MESH,
        )

    sources = (slab <= slabs - 2, slab >= 1, slab <= slabs - 3, slab >= 2)

    def stencil(turn, field):
        fields[turn] = field
        for number, (step, exists) in enumerate(steps):
            @pl.when(exists)
            def _():
                halo_copy(turn, number, step).start()

        for number, (step, exists) in enumerate(steps):
            @pl.when(sources[number])
            def _():
                halo_copy(turn, number, step).wait_recv()

        got = [jnp.where(sources[number], halos[turn, number], 0.0) for number in range(4)]
        before = jnp.where(lane == 0, pltpu.roll(got[1], 1, 1), pltpu.roll(field, 1, 1))
        after = jnp.where(lane == rows - 1, pltpu.roll(got[0], rows - 1, 1), pltpu.roll(field, rows - 1, 1))
        for number, (step, exists) in enumerate(steps):
            @pl.when(exists)
            def _():
                halo_copy(turn, number, step).wait_send()

        return 4.0 * field - before - after - got[2] - got[3]

    def summed(turn, mine):
        totals[turn, 0] = mine

        def near_copy(number):
            return pltpu.make_async_remote_copy(
                src_ref=totals.at[turn, 0],
                dst_ref=near_box.at[turn, number],
                send_sem=near_send.at[turn, number],
                recv_sem=near_recv.at[turn, number],
                device_id=near_peer(number),
                device_id_type=MESH,
            )

        for number in range(group - 1):
            near_copy(number).start()
        for number in range(group - 1):
            near_copy(number).wait()
        mine = mine + jnp.sum(near_box[turn], axis=0)
        totals[turn, 1] = mine

        def far_copy(number):
            return pltpu.make_async_remote_copy(
                src_ref=totals.at[turn, 1],
                dst_ref=far_box.at[turn, number],
                send_sem=far_send.at[turn, number],
                recv_sem=far_recv.at[turn, number],
                device_id=far_peer(number),
                device_id_type=MESH,
            )

        def start(number, carry):
            far_copy(number).start()
            return carry

        def wait(number, carry):
            far_copy(number).wait()
            return carry

        lax.fori_loop(0, fars - 1, start, 0)
        lax.fori_loop(0, fars - 1, wait, 0)
        mine = mine + jnp.sum(far_box[turn], axis=0)
        upper = jnp.sum(mine[:, :LANES], axis=1, keepdims=True)
        lower = jnp.sum(mine[:, LANES:], axis=1, keepdims=True)
        return upper / lower

    def folded(values):
        return sum(values[:, at : at + LANES] for at in range(0, rows, LANES))

    m0, m1, m2, m3, m4 = (moment_ref[number : number + 1, :] for number in range(5))
    smooth = stencil(0, stiffness * velocity)
    for turn in range(ITERS):
        linear = m0 + velocity * (m1 + m2) + 1.5 * velocity * velocity * m3 + (
            0.5 * velocity * velocity * velocity * m4
        )
        curvature = m2 + 2.0 * velocity * m3 + velocity * velocity * m4
        gradient = linear + stiffness * smooth
        direction = gradient / (curvature + 4.0 * stiffness * stiffness)
        scaled = stiffness * direction
        bent = stencil(turn + 1, scaled)
        mine = jnp.concatenate(
            [
                folded(direction * gradient),
                folded(curvature * direction * direction + scaled * bent),
            ],
            axis=1,
        )
        alpha = summed(turn, mine)
        velocity = velocity - alpha * direction
        smooth = smooth - alpha * bent
    out_ref[...] = velocity


def misfit_kernel(velocity_ref, part0_ref, part1_ref, part2_ref, out_ref, velocity_out_ref):
    rows = out_ref.shape[0]
    across = velocity_ref[...]
    velocity_out_ref[...] = across
    down = jnp.transpose(jnp.broadcast_to(across, (rows, rows)))
    for at in range(0, out_ref.shape[1], LANES):
        columns = slice(at, at + LANES)
        out_ref[:, columns] = part0_ref[:, columns] + down * (
            part1_ref[:, columns] + down * part2_ref[:, columns]
        )


def on_device(volume, velocity0, fetch_slab, fetch_row, modulus_class, modulus_table):
    rows, length = volume.shape[1:]
    slabs = 64
    parts = length // LANES
    f32 = jnp.float32
    vmem = pl.BlockSpec(memory_space=pltpu.VMEM)
    smem = pl.BlockSpec(memory_space=pltpu.SMEM)
    own_scan = volume.reshape(rows, length)
    peer = fetch_slab.reshape(2, rows)
    row = fetch_row.reshape(2, rows)
    dma = pltpu.SemaphoreType.DMA

    request, place = pl.pallas_call(
        slots_kernel,
        name="slots",
        out_shape=(
            jax.ShapeDtypeStruct((2, slabs, LANES), jnp.int32),
            jax.ShapeDtypeStruct((2, rows), jnp.int32),
        ),
        in_specs=[vmem, vmem],
        out_specs=(vmem, vmem),
    )(peer, row)

    arrived = pl.pallas_call(
        exchange_kernel,
        name="exchange",
        out_shape=jax.ShapeDtypeStruct((2, slabs, CAP, parts, LANES), f32),
        in_specs=[vmem, vmem],
        out_specs=pl.BlockSpec(memory_space=pl.ANY),
        scratch_shapes=[
            pltpu.VMEM((2, slabs, 1, LANES), jnp.int32),
            pltpu.SMEM((2, slabs, 1, LANES), jnp.int32),
            pltpu.VMEM((rows, parts, LANES), f32),
            pltpu.VMEM((2, slabs, CAP, parts, LANES), f32),
            pltpu.VMEM((slabs // 2, CAP, parts, LANES), f32),
            dma((2,)), dma((2,)), dma, dma((2,)), dma((2,)), dma((slabs // 2,)), dma,
        ],
        compiler_params=pltpu.CompilerParams(
            collective_id=0, has_side_effects=True, vmem_limit_bytes=40 * 1024 * 1024
        ),
    )(request.reshape(2, slabs, 1, LANES), own_scan)

    high, low = filter_parts()
    block = 128
    columns = pl.BlockSpec((block, length), lambda step: (step, 0))
    moments, part0, part1, part2 = pl.pallas_call(
        terms_kernel,
        name="terms",
        grid=(rows // block,),
        out_shape=(
            jax.ShapeDtypeStruct((8, rows), f32),
            jax.ShapeDtypeStruct((rows, length), f32),
            jax.ShapeDtypeStruct((rows, length), f32),
            jax.ShapeDtypeStruct((rows, length), f32),
        ),
        in_specs=[smem, vmem, columns, vmem, vmem],
        out_specs=(
            pl.BlockSpec((8, block), lambda step: (0, step)), columns, columns, columns,
        ),
        scratch_shapes=[
            pltpu.VMEM((2, block * parts, LANES), f32),
            pltpu.VMEM((2, parts, block, LANES), f32),
            pltpu.VMEM((2, parts, block, LANES), f32),
            pltpu.VMEM((5, block, LANES), f32),
        ],
        compiler_params=pltpu.CompilerParams(vmem_limit_bytes=40 * 1024 * 1024),
    )(place, arrived.reshape(2 * slabs * CAP * parts, LANES), own_scan, high, low)

    velocity = pl.pallas_call(
        descent_kernel,
        name="descent",
        out_shape=jax.ShapeDtypeStruct((1, rows), f32),
        in_specs=[smem, vmem, vmem, vmem],
        out_specs=vmem,
        scratch_shapes=[
            pltpu.VMEM((ITERS + 1, 1, rows), f32),
            pltpu.VMEM((ITERS + 1, 4, 1, rows), f32),
            pltpu.VMEM((ITERS, 2, 1, 2 * LANES), f32),
            pltpu.VMEM((ITERS, 7, 1, 2 * LANES), f32),
            pltpu.VMEM((ITERS, 31, 1, 2 * LANES), f32),
            dma((ITERS + 1, 4)), dma((ITERS + 1, 4)),
            dma((ITERS, 7)), dma((ITERS, 7)), dma((ITERS, 31)), dma((ITERS, 31)),
        ],
        compiler_params=pltpu.CompilerParams(collective_id=1, has_side_effects=True),
    )(modulus_table, moments, velocity0, modulus_class)

    misfit, velocity = pl.pallas_call(
        misfit_kernel,
        name="misfit",
        grid=(rows // block,),
        out_shape=(
            jax.ShapeDtypeStruct((rows, length), f32),
            jax.ShapeDtypeStruct((1, rows), f32),
        ),
        in_specs=[
            pl.BlockSpec((1, block), lambda step: (0, step)), columns, columns, columns,
        ],
        out_specs=(columns, pl.BlockSpec((1, block), lambda step: (0, step))),
    )(velocity, part0, part1, part2)
    return velocity, misfit.reshape(volume.shape)


def solution(mesh):
    return jax.shard_map(
        on_device,
        mesh=mesh,
        in_specs=(
            P("scan", "slab", None),
            P("scan", "slab"),
            P("scan", None, "slab", None),
            P("scan", None, "slab"),
            P("scan", "slab"),
            P(),
        ),
        out_specs=(P("scan", "slab"), P("scan", "slab", None)),
        check_vma=False,
    )
```

time: 541 us -> 215 us (0.40)
  Pallas kernels: 0 us -> 203 us
  blocking collectives: 190 us -> 0 us
  waiting for transfers between devices: 128 us -> 0 us
  starting transfers between devices: 81.7 us -> 0 us
  local copies, waits for them, and re-layouts: 77.3 us -> 11 us
  other arithmetic: 38.1 us -> 0 us
  matrix products: 17 us -> 0 us
    pallas_call x0 -> x5, Pallas kernels: none -> 203 us  [the longest x1 131 us: on_device(): pl.pallas_call(exchange_kernel, name='exchange', out_shape=jax.ShapeDtype...]
    psum x2 -> x0, blocking collectives: 167 us -> none  [on_device(): lax.psum((jnp.sum(direction * gradient), jnp.sum(curvature * direction *...]
    all_to_all x1 -> x0, waiting for transfers between devices: 114 us -> none  [on_device(): lax.all_to_all(jnp.stack([forward_rows, backward_rows]), 'slab', split_ax...]
    ppermute x18 -> x0, starting transfers between devices: 66.4 us -> none  [the longest x10 23.7 us: passed_along(): return lax.ppermute(block, axis, route)]
    gather x5 -> x0, local copies, waits for them, and re-layouts: 38 us -> none  [the longest x1 21.5 us: on_device(): fetched = arrived[direction_ids, peer_ids, slot_ids]]
    all_to_all x1 -> x0, blocking collectives: 23.1 us -> none  [on_device(): lax.all_to_all(request_table, 'slab', split_axis=1, concat_axis=1, tiled=...]
    dot_general x8 -> x0, matrix products: 17 us -> none  [prefilter(): jnp.dot(window, matrix, preferred_element_type=jnp.float32, precision=lax...]
    all_to_all x1 -> x0, starting transfers between devices: 15.3 us -> none  [on_device(): lax.all_to_all(jnp.stack([forward_rows, backward_rows]), 'slab', split_ax...]
  transfers between devices with their start and end apart: 19 -> 0, of which waited for: 4 -> 0; matrix products, arithmetic and copies ran while one was open for 16% -> 0% of each run, Pallas kernels for 0% -> 0%
where the time goes in v1:
time: 215 us; the launch traced here: 214 us
  Pallas kernels  203 us (94%)
  local copies, waits for them, and re-layouts  11 us (5%)
    pallas_call x1, Pallas kernels, on_device(): pl.pallas_call(exchange_kernel, name='exchange', out_shape=jax.ShapeDtype...  131 us
    pallas_call x1, Pallas kernels, on_device(): pl.pallas_call(descent_kernel, name='descent', out_shape=jax.ShapeDtypeSt...  43.8 us
    pallas_call x1, Pallas kernels, on_device(): pl.pallas_call(terms_kernel, name='terms', grid=(rows // block,), out_sha...  21.8 us
    unnamed x23, local copies, waits for them, and re-layouts  11 us
    pallas_call x1, Pallas kernels, on_device(): pl.pallas_call(misfit_kernel, name='misfit', grid=(rows // block,), out_s...  4.78 us

profile of v1, /device:TPU:1, one launch (start us, length us, event | category | flops | bytes accessed | tf_op | source)
XLA Modules:
  0.0 214.5 jit_solution(18251495832099989483)
XLA Ops:
  0.6 1.3 copy.12
  1.9 2.1 slots.1
  4.0 0.0 copy-start.1
  4.0 1.6 copy-done.1
  5.6 0.0 copy-start.8
  5.6 0.8 copy-done.8
  6.4 0.0 copy-start.2
  6.4 0.0 copy-start.7
  6.4 0.0 copy-start.10
  6.4 130.5 %exchange.1 = f32[2,64,12,8,128]{4,3,2,1,0:T(8,128)S(1)} custom-call(s32[2,64,1,128]{3,2,1,0:T(1,128)S(1)} %bitcast.11, f32[512,1024]{1,0:T(8,128)S(1)} %bitcast.9), custom_call_target="tpu_custom_call" | custom-call | tf_op jit(solution)/shard_map/exchange/pallas_call | solution.py:568
  136.9 0.0 copy-start
  136.9 2.6 %copy-done = f32[2,64,12,8,128]{4,3,2,1,0:T(8,128)} copy-done((f32[2,64,12,8,128]{4,3,2,1,0:T(8,128)}, f32[2,64,12,8,128]{4,3,2,1,0:T(8,128)S(1)}, u32[]{:S(2)}) %copy-start) | copy-done | bytes 6291480
  139.6 0.0 copy-done.2
  139.6 0.0 copy-done.6
  139.6 0.0 copy-done.7
  139.6 0.0 copy-done.10
  139.6 21.8 %terms.1 = (f32[8,512]{1,0:T(8,128)S(1)}, f32[512,1024]{1,0:T(8,128)S(1)}, f32[512,1024]{1,0:T(8,128)S(1)}, f32[512,1024]{1,0:T(8,128)S(1)}) custom-call(s32[2,512]{1,0:T(2,128)S(1)} %copy-done.10, f32[12288,128]{1,0:T(8,128)} %bitcast.8, f32[512,1024]{1,0:T(8,128)S(1)} %bitcast.10, bf16[128,256]{1,0:T(8,128)(2,1)S(1)} %copy-done.7, ...), custom_call_target="tpu_custom_call" | custom-call | tf_op jit(solution)/shard_map/terms/pallas_call | solution.py:590
  161.3 0.0 copy-start.3
  161.3 1.4 copy-done.3
  162.7 1.3 copy-done.4
  164.0 1.3 copy-done.5
  165.3 0.6 copy-done.9
  165.9 43.8 %descent.1.velocity_ref = f32[1,512]{1,0:T(1,128)} custom-call(f32[4]{0:T(128)} %table_ref.1, f32[8,512]{1,0:T(8,128)} %copy-done.9, f32[1,512]{1,0:T(1,128)} %velocity_ref.1, s32[1,512]{1,0:T(1,128)} %class_ref.1), custom_call_target="tpu_custom_call" | custom-call | tf_op jit(solution)/shard_map/descent/pallas_call | solution.py:613
  209.7 4.8 %misfit.1 = (f32[512,1024]{1,0:T(8,128)}, f32[1,512]{1,0:T(1,128)}) custom-call(f32[1,512]{1,0:T(1,128)} %descent.1.velocity_ref, f32[512,1024]{1,0:T(8,128)} %copy-done.3, f32[512,1024]{1,0:T(8,128)} %copy-done.4, f32[512,1024]{1,0:T(8,128)} %copy-done.5), custom_call_target="tpu_custom_call" | custom-call | tf_op jit(solution)/shard_map/misfit/pallas_call | solution.py:631
  (4 shorter events, 0.0 us)
Async XLA Ops:
  4.0 1.6 copy-start.1
  5.6 0.8 copy-start.8
  6.4 133.2 %copy-start.2 = (f32[1,512,1024]{2,1,0:T(8,128)S(1)}, f32[1,512,1024]{2,1,0:T(8,128)}, u32[]{:S(2)}) copy-start(f32[1,512,1024]{2,1,0:T(8,128)} %param.8) | copy-start | bytes 6291460
  6.4 133.2 %copy-start.6 = (bf16[128,256]{1,0:T(8,128)(2,1)S(1)}, bf16[128,256]{1,0:T(8,128)(2,1)}, u32[]{:S(2)}) copy-start(bf16[128,256]{1,0:T(8,128)(2,1)} %constant.5.clone.low_ref) | copy-start | bytes 196612
  6.4 133.2 %copy-start.7 = (bf16[128,256]{1,0:T(8,128)(2,1)S(1)}, bf16[128,256]{1,0:T(8,128)(2,1)}, u32[]{:S(2)}) copy-start(bf16[128,256]{1,0:T(8,128)(2,1)} %constant.4.clone.high_ref) | copy-start | bytes 196612
  6.4 133.2 %copy-start.10 = (s32[2,512]{1,0:T(2,128)S(1)}, s32[2,512]{1,0:T(2,128)}, u32[]{:S(2)}) copy-start(s32[2,512]{1,0:T(2,128)} %get-tuple-element.10.place_ref) | copy-start | bytes 12292
  136.9 2.6 %copy-start = (f32[2,64,12,8,128]{4,3,2,1,0:T(8,128)}, f32[2,64,12,8,128]{4,3,2,1,0:T(8,128)S(1)}, u32[]{:S(2)}) copy-start(f32[2,64,12,8,128]{4,3,2,1,0:T(8,128)S(1)} %exchange.1) | copy-start | bytes 18874372
  161.3 1.4 copy-start.3
  162.7 1.3 copy-start.4
  164.0 1.3 copy-start.5
  165.3 0.6 copy-start.9

commit v2 on v0

v2 whole, which is shorter than its diff:
```python
import math

import jax
import jax.numpy as jnp
import numpy as np
from jax import lax
from jax.experimental import pallas as pl
from jax.experimental.pallas import tpu as pltpu
from jax.sharding import PartitionSpec as P

BAND = 32
ITERS = 2
CAP = 12
LANES = 128
SCANS = 4
SLABS = 64
LAYERS = 8
BATCH = 4
MESH = pl.DeviceIdType.MESH
MIB = 1024 * 1024

root_three = math.sqrt(3.0)
pole_value = math.sqrt(3.0) - 2.0


def filter_parts():
    source = np.arange(LANES)[:, None]
    column = np.arange(2 * LANES)[None, :]
    lane = column % LANES
    beside = np.where(lane < LANES // 2, lane + LANES, lane - LANES)
    distance = np.abs(source - np.where(column < LANES, lane, beside))
    matrix = np.where(distance <= BAND, root_three * pole_value ** distance, 0.0)
    matrix = matrix.astype(np.float32)
    high = matrix.astype(jnp.bfloat16)
    low = (matrix - high.astype(np.float32)).astype(jnp.bfloat16)
    return jnp.asarray(np.concatenate([high, high])), jnp.asarray(low)


def shifts(number):
    phase = number % 8
    wave = number // 8
    shift_z = jnp.where(phase % 2 == 0, (8 - phase // 2) % 8, (phase + 1) // 2)
    return shift_z, 2 * (wave % 2) + wave // 4, (wave // 2) % 2


def displaced(slab, number):
    shift_z, shift_x, shift_c = shifts(number)
    core = (slab % 2 + shift_c) % 2
    at_x = ((slab // 2) % 4 + shift_x) % 4
    at_z = (slab // 8 + shift_z) % 8
    return (at_z * 4 + at_x) * 2 + core


def number_between(source, target):
    shift_c = (target % 2 + 2 - source % 2) % 2
    shift_x = ((target // 2) % 4 + 4 - (source // 2) % 4) % 4
    shift_z = (target // 8 + 8 - source // 8) % 8
    phase = jnp.where(shift_z > 4, 2 * (8 - shift_z), jnp.maximum(2 * shift_z - 1, 0))
    wave = shift_x // 2 + 2 * shift_c + 4 * (shift_x % 2)
    return wave * 8 + phase


def slots_kernel(peer_ref, row_ref, request_ref, wanting_ref, place_ref):
    slab = lax.axis_index("slab")
    rows = peer_ref.shape[1]
    earlier = (
        lax.broadcasted_iota(jnp.int32, (rows, rows), 0)
        < lax.broadcasted_iota(jnp.int32, (rows, rows), 1)
    ).astype(jnp.float32).astype(jnp.bfloat16)
    contract = (((1,), (1,)), ((), ()))
    here = lax.broadcasted_iota(jnp.int32, (1, rows), 1)
    for side in range(2):
        peer = peer_ref[side : side + 1, :]
        named = (lax.broadcasted_iota(jnp.int32, (SLABS, rows), 0) == peer).astype(jnp.float32)
        named16 = named.astype(jnp.bfloat16)
        before = jnp.dot(named16, earlier, preferred_element_type=jnp.float32)
        slot = jnp.sum(before * named, axis=0, keepdims=True).astype(jnp.int32)
        at_slot = (lax.broadcasted_iota(jnp.int32, (LANES, rows), 0) == slot).astype(jnp.float32)

        def tabled(numbers):
            high = (at_slot * (numbers // 16).astype(jnp.float32)).astype(jnp.bfloat16)
            low = (at_slot * (numbers % 16).astype(jnp.float32)).astype(jnp.bfloat16)
            return (
                16.0 * lax.dot_general(named16, high, contract, preferred_element_type=jnp.float32)
                + lax.dot_general(named16, low, contract, preferred_element_type=jnp.float32)
            ).astype(jnp.int32)

        request_ref[side] = tabled(row_ref[side : side + 1, :])
        wanting_ref[side] = tabled(here)
        place_ref[side : side + 1, :] = number_between(peer, slab) * CAP + jnp.minimum(slot, CAP - 1)


def velocity_kernel(
    table_ref, wanting_scalar, place_scalar, request, place, volume_ref, velocity_ref, class_ref,
    high_ref, low_ref,
    out_ref, part0_ref, part1_ref, part2_ref,
    volume, by_row, asked, asked_scalar,
    packed, relay, arrived, value, slope, bend, middle, beside, own, sums, chosen, parts_buf,
    near_box, far_box, totals,
    volume_sem, ask_send, ask_recv, scalar_sem, row_send, row_recv, relay_recv, relay_send,
    near_send, near_recv, far_send, far_recv, part_sem,
):
    scan = lax.axis_index("scan")
    slab = lax.axis_index("slab")
    rows = velocity_ref.shape[1]
    blocks = volume_ref.shape[1] // LANES
    group = SLABS // LAYERS
    position = slab % group
    layer = slab // group
    fars = SCANS * LAYERS
    last = SCANS - 1
    edge = jnp.logical_or(scan == 0, scan == last)
    down = scan >= 1
    up = scan <= last - 1
    present = (up, down)

    volume_copy = pltpu.make_async_copy(volume_ref, volume, volume_sem)
    volume_copy.start()

    barrier = pltpu.get_barrier_semaphore()

    def near_peer(number):
        return (scan, layer * group + (position + 1 + number) % group)

    def far_peer(number):
        other = (scan * LAYERS + layer + 1 + number) % fars
        return (other // LAYERS, (other % LAYERS) * group + position)

    below = jnp.logical_and(layer >= 1, position <= 1)
    above = layer <= LAYERS - 2
    to_above = jnp.logical_and(above, position >= group - 2)

    def greet(device):
        pl.semaphore_signal(barrier, inc=1, device_id=device, device_id_type=MESH)

    def greet_rows(number, carry):
        @pl.when(down)
        def _():
            greet((scan - 1, number))

        @pl.when(up)
        def _():
            greet((scan + 1, number))

        @pl.when(jnp.logical_and(edge, number != slab))
        def _():
            greet((scan, number))

        return carry

    def greet_far(number, carry):
        greet(far_peer(number))
        return carry

    lax.fori_loop(0, SLABS, greet_rows, 0)
    lax.fori_loop(0, fars - 1, greet_far, 0)
    for number in range(group - 1):
        greet(near_peer(number))

    @pl.when(above)
    def _():
        for number in range(2):
            greet((scan, (layer + 1) * group + number))

    @pl.when(below)
    def _():
        for number in range(group):
            greet((scan, (layer - 1) * group + number))

    expected = (
        jnp.where(edge, 2 * SLABS - 1, 2 * SLABS) + fars - 1 + group - 1
        + jnp.where(above, 2, 0) + jnp.where(below, group, 0)
    )

    volume_copy.wait()

    def relayout(block, carry):
        base = pl.multiple_of(block * 8, 8)
        for part in range(blocks):
            by_row[pl.ds(base, 8), part, :] = volume[
                pl.ds(base, 8), part * LANES : (part + 1) * LANES
            ]
        return carry

    lax.fori_loop(0, rows // 8, relayout, 0)
    pl.semaphore_wait(barrier, expected)

    def ask_copy(side, number):
        return pltpu.make_async_remote_copy(
            src_ref=request.at[side, number],
            dst_ref=asked.at[side, slab],
            send_sem=ask_send.at[side],
            recv_sem=ask_recv.at[side],
            device_id=(scan + 1 - 2 * side, number),
            device_id_type=MESH,
        )

    def ask(number, carry):
        target = displaced(slab, number)

        @pl.when(up)
        def _():
            ask_copy(0, target).start()

        @pl.when(down)
        def _():
            ask_copy(1, target).start()

        return carry

    lax.fori_loop(0, SLABS, ask, 0)

    def whole_ask(side):
        return pltpu.make_async_remote_copy(
            src_ref=request.at[side],
            dst_ref=asked.at[side],
            send_sem=ask_send.at[side],
            recv_sem=ask_recv.at[side],
            device_id=(scan, slab),
            device_id_type=MESH,
        )

    def near_copy(turn, index, entry, device):
        return pltpu.make_async_remote_copy(
            src_ref=near_box.at[turn, position + 2],
            dst_ref=near_box.at[turn, entry],
            send_sem=near_send.at[turn, index],
            recv_sem=near_recv.at[turn, entry],
            device_id=device,
            device_id_type=MESH,
        )

    def shares(turn, act):
        for number in range(group - 1):
            act(near_copy(turn, number, position + 2, near_peer(number)))

        @pl.when(below)
        def _():
            for number in range(group):
                act(near_copy(turn, 7 + number, position + group + 2, (scan, (layer - 1) * group + number)))

        @pl.when(to_above)
        def _():
            for number in range(2):
                act(near_copy(turn, 7 + number, position - group + 2, (scan, (layer + 1) * group + number)))

    def share(turn, message):
        near_box[turn, position + 2] = message
        shares(turn, lambda copy: copy.start())

    def collect(turn):
        def wait(entry):
            near_copy(turn, 0, entry, (scan, slab)).wait_recv()

        for entry in range(2, group + 2):
            @pl.when(position + 2 != entry)
            def _():
                wait(entry)

        @pl.when(above)
        def _():
            wait(group + 2)
            wait(group + 3)

        @pl.when(below)
        def _():
            wait(0)
            wait(1)

        shares(turn, lambda copy: copy.wait_send())

    lane_row = lax.broadcasted_iota(jnp.int32, (1, rows), 1)

    def stencil(turn, field):
        def entry(offset):
            return near_box[turn, position + 2 + offset, :, :rows]

        lower1 = jnp.where(slab >= 1, entry(-1), 0.0)
        lower2 = jnp.where(slab >= 2, entry(-2), 0.0)
        upper1 = jnp.where(slab <= SLABS - 2, entry(1), 0.0)
        upper2 = jnp.where(slab <= SLABS - 3, entry(2), 0.0)
        left = jnp.where(lane_row == 0, pltpu.roll(lower1, 1, 1), pltpu.roll(field, 1, 1))
        right = jnp.where(
            lane_row == rows - 1, pltpu.roll(upper1, rows - 1, 1), pltpu.roll(field, rows - 1, 1)
        )
        return 4.0 * field - left - right - lower2 - upper2

    weight = jnp.zeros((1, rows), jnp.float32)
    for number in range(4):
        weight = jnp.where(class_ref[...] == number, table_ref[number], weight)
    stiffness = jnp.sqrt(weight)
    velocity = velocity_ref[...]
    blank = jnp.zeros((1, 2 * LANES), jnp.float32)
    share(0, jnp.concatenate([stiffness * velocity, blank], axis=1))

    def take_asked(side):
        whole_ask(side).wait_recv()
        copy = pltpu.make_async_copy(asked.at[side], asked_scalar.at[side], scalar_sem)
        copy.start()
        copy.wait()

    @pl.when(down)
    def _():
        take_asked(0)

    @pl.when(up)
    def _():
        take_asked(1)

    def row_copy(source, side, number, target, target_scan, send_sem):
        return pltpu.make_async_remote_copy(
            src_ref=source,
            dst_ref=arrived.at[side, number],
            send_sem=send_sem,
            recv_sem=row_recv.at[side, number],
            device_id=(target_scan, target),
            device_id_type=MESH,
        )

    def relay_copy(side, number, relay_number, target_scan):
        return pltpu.make_async_remote_copy(
            src_ref=packed.at[side, number],
            dst_ref=relay.at[relay_number],
            send_sem=row_send.at[side],
            recv_sem=relay_recv.at[relay_number],
            device_id=(target_scan, slab),
            device_id_type=MESH,
        )

    def serve(side, number, target, relayed_scan):
        target_scan = scan - 1 + 2 * side
        relay_number = (number // 16) * 8 + number % 8
        relayed = jnp.logical_and(scan == relayed_scan, (number // 8) % 2 == 1)
        for slot in range(CAP):
            packed[side, number, slot] = by_row[asked_scalar[side, target, 0, slot]]

        @pl.when(relayed)
        def _():
            relay_copy(side, number, relay_number, target_scan).start()

        @pl.when(jnp.logical_not(relayed))
        def _():
            row_copy(
                packed.at[side, number], side, number, target, target_scan, row_send.at[side]
            ).start()

    def send(number, carry):
        target = displaced(slab, number)

        @pl.when(down)
        def _():
            serve(0, number, target, 1)

        @pl.when(up)
        def _():
            serve(1, number, target, 2)

        return carry

    lax.fori_loop(0, SLABS, send, 0)

    for side in range(2):
        across = place[side : side + 1, :].astype(jnp.float32)
        upright = jnp.transpose(jnp.broadcast_to(across, (LANES, rows)))
        lane = lax.broadcasted_iota(jnp.int32, (rows, LANES), 1).astype(jnp.float32)
        for block in range(SLABS * CAP // LANES):
            at = side * SLABS * CAP + block * LANES
            chosen[:, at : at + LANES] = (
                (upright == lane + float(block * LANES)).astype(jnp.float32).astype(jnp.bfloat16)
            )

        @pl.when(jnp.logical_not(present[side]))
        def _():
            sums[side] = jnp.zeros(sums.shape[1:], jnp.float32)

    collect(0)
    smooth = stencil(0, stiffness * velocity)

    lane8 = lax.broadcasted_iota(jnp.int32, (8, LANES), 1)
    zero8 = jnp.zeros((8, LANES), jnp.float32)
    batch_rows = BATCH * CAP

    def absorb(side, batch):
        for one in range(BATCH):
            number = batch * BATCH + one
            row_copy(packed.at[side, number], side, number, slab, scan, row_send.at[side]).wait_recv()
        voxels = arrived[side, pl.ds(batch * BATCH, BATCH)].reshape(batch_rows * blocks, LANES)
        top = voxels.astype(jnp.bfloat16)
        rest = (voxels - top.astype(jnp.float32)).astype(jnp.bfloat16)
        both = jnp.dot(
            jnp.concatenate([top, rest], axis=1), high_ref[...], preferred_element_type=jnp.float32
        ) + jnp.dot(top, low_ref[...], preferred_element_type=jnp.float32)
        middle[...] = both[:, :LANES].reshape(batch_rows, blocks, LANES)
        beside[...] = both[:, LANES:].reshape(batch_rows, blocks, LANES)
        for chunk in range(BATCH):
            source = displaced_back(batch * BATCH + chunk)
            for slot in range(CAP):
                own[chunk * CAP + slot] = by_row[wanting_scalar[side, source, slot]]

        def combine(eight, carry):
            at = pl.ds(pl.multiple_of(eight * 8, 8), 8)
            to = pl.ds(pl.multiple_of(batch * batch_rows + eight * 8, 8), 8)
            coeffs = []
            for block in range(blocks):
                left = beside[at, block - 1, :] if block > 0 else zero8
                right = beside[at, block + 1, :] if block < blocks - 1 else zero8
                coeffs.append(middle[at, block, :] + jnp.where(lane8 < LANES // 2, left, right))
            to_right = [pltpu.roll(one, 1, 1) for one in coeffs]
            to_left = [pltpu.roll(one, LANES - 1, 1) for one in coeffs]
            total = [zero8] * 5
            for block in range(blocks):
                prior = jnp.where(lane8 == 0, to_right[block - 1] if block > 0 else zero8, to_right[block])
                after = jnp.where(
                    lane8 == LANES - 1,
                    to_left[block + 1] if block < blocks - 1 else zero8,
                    to_left[block],
                )
                ends = prior + after
                v = (ends + 4.0 * coeffs[block]) * (1.0 / 6.0)
                s = 0.5 * (after - prior)
                b = ends - 2.0 * coeffs[block]
                off = v - own[at, block, :]
                value[side, to, block, :] = v
                slope[side, to, block, :] = s
                bend[side, to, block, :] = b
                total[0] += s * off
                total[1] += b * off
                total[2] += s * s
                total[3] += s * b
                total[4] += b * b
            column = zero8
            for number in range(5):
                summed = jnp.sum(total[number], axis=1, keepdims=True)
                if side == 1 and number in (0, 3):
                    summed = -summed
                column = jnp.where(lane8 % 8 == number, summed, column)
            first = column.astype(jnp.bfloat16).astype(jnp.float32)
            second = (column - first).astype(jnp.bfloat16).astype(jnp.float32)
            third = (column - first - second).astype(jnp.bfloat16).astype(jnp.float32)
            column = jnp.where(lane8 < 8, first, jnp.where(lane8 < 16, second, third))
            sums[side, to, :] = jnp.where(lane8 < 24, column, 0.0)
            return carry

        lax.fori_loop(0, batch_rows // 8, combine, 0)

    def displaced_back(number):
        shift_z, shift_x, shift_c = shifts(number)
        core = (slab % 2 + 2 - shift_c) % 2
        at_x = ((slab // 2) % 4 + 4 - shift_x) % 4
        at_z = (slab // 8 + 8 - shift_z) % 8
        return (at_z * 4 + at_x) * 2 + core

    def pass_on(side, relay_number):
        number = (relay_number // 8) * 16 + 8 + relay_number % 8
        relay_copy(side, number, relay_number, scan).wait_recv()
        row_copy(
            relay.at[relay_number], side, number, displaced(slab, number), scan, relay_send
        ).start()

    def step(batch, carry):
        for side, relaying in ((0, scan == 0), (1, scan == last)):
            @pl.when(jnp.logical_and(relaying, batch < SLABS // 8))
            def _():
                for one in range(4):
                    pass_on(side, batch * 4 + one)

        for side in range(2):
            @pl.when(present[side])
            def _():
                absorb(side, batch)

        return carry

    lax.fori_loop(0, SLABS // BATCH, step, 0)

    moments = jnp.dot(
        chosen[...],
        sums[...].reshape(2 * SLABS * CAP, LANES).astype(jnp.bfloat16),
        preferred_element_type=jnp.float32,
    )
    moments = jnp.transpose(moments)
    moments = moments[0:8] + moments[8:16] + moments[16:24]
    m0, m1, m2, m3, m4 = (moments[number : number + 1, :] for number in range(5))

    def coefficients(quarter):
        def one_row(row):
            forward = place_scalar[0, row]
            backward = place_scalar[1, row]

            def got(ref):
                return (
                    jnp.where(up, ref[0, forward], 0.0),
                    jnp.where(down, ref[1, backward], 0.0),
                )

            value_f, value_b = got(value)
            slope_f, slope_b = got(slope)
            bend_f, bend_b = got(bend)
            parts_buf[0, row] = value_f + value_b - 2.0 * by_row[row]
            parts_buf[1, row] = slope_f - slope_b
            parts_buf[2, row] = 0.5 * (bend_f + bend_b)

        def four(step, carry):
            for one in range(4):
                one_row(quarter * (rows // 4) + step * 4 + one)
            return carry

        lax.fori_loop(0, rows // 16, four, 0)
        for copy in part_copies(quarter):
            copy.start()

    def part_copies(quarter):
        at = pl.ds(quarter * (rows // 4), rows // 4)
        return [
            pltpu.make_async_copy(parts_buf.at[number, at], ref.at[at], part_sem.at[number, quarter])
            for number, ref in enumerate((part0_ref, part1_ref, part2_ref))
        ]

    def folded(values):
        return sum(values[:, at : at + LANES] for at in range(0, rows, LANES))

    for turn in range(ITERS):
        linear = m0 + velocity * (m1 + m2) + 1.5 * velocity * velocity * m3 + (
            0.5 * velocity * velocity * velocity * m4
        )
        curvature = m2 + 2.0 * velocity * m3 + velocity * velocity * m4
        gradient = linear + stiffness * smooth
        direction = gradient / (curvature + 4.0 * stiffness * stiffness)
        scaled = stiffness * direction
        share(
            turn + 1,
            jnp.concatenate(
                [
                    scaled,
                    folded(direction * gradient),
                    folded(curvature * direction * direction + 4.0 * scaled * scaled),
                ],
                axis=1,
            ),
        )
        coefficients(2 * turn)
        collect(turn + 1)
        box = near_box[turn + 1, :, 0, :]
        fields = box[2 : group + 2, :rows]
        beyond = jnp.where(
            jnp.logical_or(above, lax.broadcasted_iota(jnp.int32, (4, rows), 0) < 2),
            box[group : group + 4, :rows], 0.0,
        )
        next1 = jnp.concatenate([box[3 : group + 2, :rows], beyond[2:3]], axis=0)
        next2 = jnp.concatenate([box[4 : group + 2, :rows], beyond[2:4]], axis=0)
        lane_all = lax.broadcasted_iota(jnp.int32, (group, rows), 1)
        right = jnp.where(
            lane_all == rows - 1, pltpu.roll(next1, rows - 1, 1), pltpu.roll(fields, rows - 1, 1)
        )
        cross = jnp.sum(folded(fields * (right + next2)), axis=0, keepdims=True)
        mine = jnp.sum(box[2 : group + 2, rows:], axis=0, keepdims=True)
        mine = mine - jnp.concatenate([jnp.zeros_like(cross), 2.0 * cross], axis=1)
        totals[turn] = mine

        def far_copy(number):
            return pltpu.make_async_remote_copy(
                src_ref=totals.at[turn],
                dst_ref=far_box.at[turn, number],
                send_sem=far_send.at[turn, number],
                recv_sem=far_recv.at[turn, number],
                device_id=far_peer(number),
                device_id_type=MESH,
            )

        def far_start(number, carry):
            far_copy(number).start()
            return carry

        def far_wait(number, carry):
            far_copy(number).wait()
            return carry

        lax.fori_loop(0, fars - 1, far_start, 0)
        bent = stencil(turn + 1, scaled)
        coefficients(2 * turn + 1)
        lax.fori_loop(0, fars - 1, far_wait, 0)
        mine = mine + jnp.sum(far_box[turn], axis=0)
        upper = jnp.sum(mine[:, :LANES], axis=1, keepdims=True)
        lower = jnp.sum(mine[:, LANES:], axis=1, keepdims=True)
        alpha = upper / lower
        velocity = velocity - alpha * direction
        smooth = smooth - alpha * bent
    out_ref[...] = velocity

    @pl.when(up)
    def _():
        whole_ask(0).wait_send()

    @pl.when(down)
    def _():
        whole_ask(1).wait_send()

    for side, serving in ((0, down), (1, up)):
        @pl.when(serving)
        def _():
            pltpu.make_async_remote_copy(
                src_ref=packed.at[side],
                dst_ref=arrived.at[side],
                send_sem=row_send.at[side],
                recv_sem=row_recv.at[side, 0],
                device_id=(scan, slab),
                device_id_type=MESH,
            ).wait_send()

    @pl.when(edge)
    def _():
        pltpu.make_async_remote_copy(
            src_ref=relay,
            dst_ref=relay,
            send_sem=relay_send,
            recv_sem=relay_recv.at[0],
            device_id=(scan, slab),
            device_id_type=MESH,
        ).wait_send()

    for quarter in range(4):
        for copy in part_copies(quarter):
            copy.wait()


def misfit_kernel(velocity_ref, part0_ref, part1_ref, part2_ref, out_ref, velocity_out_ref, upright):
    rows = out_ref.shape[0]
    across = velocity_ref[...]
    velocity_out_ref[...] = across
    upright[...] = jnp.transpose(jnp.broadcast_to(across, (rows, rows)))

    def eight(step, carry):
        at = pl.ds(pl.multiple_of(step * 8, 8), 8)
        moved = upright[at, :]
        for block in range(out_ref.shape[1] // LANES):
            out_ref[at, block * LANES : (block + 1) * LANES] = part0_ref[at, block, :] + moved * (
                part1_ref[at, block, :] + moved * part2_ref[at, block, :]
            )
        return carry

    lax.fori_loop(0, rows // 8, eight, 0, unroll=2)


def on_device(volume, velocity0, fetch_slab, fetch_row, modulus_class, modulus_table):
    rows, length = volume.shape[1:]
    blocks = length // LANES
    f32 = jnp.float32
    i32 = jnp.int32
    vmem = pl.BlockSpec(memory_space=pltpu.VMEM)
    smem = pl.BlockSpec(memory_space=pltpu.SMEM)
    anywhere = pl.BlockSpec(memory_space=pl.ANY)
    dma = pltpu.SemaphoreType.DMA
    high, low = filter_parts()
    tile = (blocks, LANES)
    turns = ITERS + 1
    wide = rows + 2 * LANES

    request, wanting, place = pl.pallas_call(
        slots_kernel,
        name="slots",
        out_shape=(
            jax.ShapeDtypeStruct((2, SLABS, LANES), i32),
            jax.ShapeDtypeStruct((2, SLABS, LANES), i32),
            jax.ShapeDtypeStruct((2, rows), i32),
        ),
        in_specs=[vmem, vmem],
        out_specs=(vmem, vmem, vmem),
    )(fetch_slab.reshape(2, rows), fetch_row.reshape(2, rows))

    velocity, part0, part1, part2 = pl.pallas_call(
        velocity_kernel,
        name="velocity",
        out_shape=(
            jax.ShapeDtypeStruct((1, rows), f32),
            jax.ShapeDtypeStruct((rows,) + tile, f32),
            jax.ShapeDtypeStruct((rows,) + tile, f32),
            jax.ShapeDtypeStruct((rows,) + tile, f32),
        ),
        in_specs=[smem, smem, smem, vmem, vmem, anywhere, vmem, vmem, vmem, vmem],
        out_specs=(vmem, anywhere, anywhere, anywhere),
        scratch_shapes=[
            pltpu.VMEM((rows, length), f32),
            pltpu.VMEM((rows,) + tile, f32),
            pltpu.VMEM((2, SLABS, 1, LANES), i32),
            pltpu.SMEM((2, SLABS, 1, LANES), i32),
            pltpu.VMEM((2, SLABS, CAP) + tile, f32),
            pltpu.VMEM((SLABS // 2, CAP) + tile, f32),
            pltpu.VMEM((2, SLABS, CAP) + tile, f32),
            pltpu.VMEM((2, SLABS * CAP) + tile, f32),
            pltpu.VMEM((2, SLABS * CAP) + tile, f32),
            pltpu.VMEM((2, SLABS * CAP) + tile, f32),
            pltpu.VMEM((BATCH * CAP,) + tile, f32),
            pltpu.VMEM((BATCH * CAP,) + tile, f32),
            pltpu.VMEM((BATCH * CAP,) + tile, f32),
            pltpu.VMEM((2, SLABS * CAP, LANES), f32),
            pltpu.VMEM((rows, 2 * SLABS * CAP), jnp.bfloat16),
            pltpu.VMEM((3, rows) + tile, f32),
            pltpu.VMEM((turns, 12, 1, wide), f32),
            pltpu.VMEM((ITERS, SCANS * LAYERS - 1, 1, 2 * LANES), f32),
            pltpu.VMEM((ITERS, 1, 2 * LANES), f32),
            dma, dma((2,)), dma((2,)), dma, dma((2,)), dma((2, SLABS)),
            dma((SLABS // 2,)), dma,
            dma((turns, 15)), dma((turns, 12)),
            dma((ITERS, SCANS * LAYERS - 1)), dma((ITERS, SCANS * LAYERS - 1)),
            dma((3, 4)),
        ],
        compiler_params=pltpu.CompilerParams(
            collective_id=0, has_side_effects=True, vmem_limit_bytes=56 * MIB
        ),
    )(
        modulus_table, wanting, place, request.reshape(2, SLABS, 1, LANES), place,
        volume.reshape(rows, length), velocity0, modulus_class, high, low,
    )

    block = 128
    across = pl.BlockSpec((1, block), lambda step: (0, step))
    tiles = pl.BlockSpec((block,) + tile, lambda step: (step, 0, 0))
    misfit, velocity = pl.pallas_call(
        misfit_kernel,
        name="misfit",
        grid=(rows // block,),
        out_shape=(
            jax.ShapeDtypeStruct((rows, length), f32),
            jax.ShapeDtypeStruct((1, rows), f32),
        ),
        in_specs=[across, tiles, tiles, tiles],
        out_specs=(pl.BlockSpec((block, length), lambda step: (step, 0)), across),
        scratch_shapes=[pltpu.VMEM((block, block), f32)],
    )(velocity, part0, part1, part2)
    return velocity, misfit.reshape(volume.shape)


def solution(mesh):
    return jax.shard_map(
        on_device,
        mesh=mesh,
        in_specs=(
            P("scan", "slab", None),
            P("scan", "slab"),
            P("scan", None, "slab", None),
            P("scan", None, "slab"),
            P("scan", "slab"),
            P(),
        ),
        out_specs=(P("scan", "slab"), P("scan", "slab", None)),
        check_vma=False,
    )
```

time: 541 us -> 182 us (0.34)
  blocking collectives: 190 us -> 0 us
  Pallas kernels: 0 us -> 180 us
  waiting for transfers between devices: 128 us -> 0 us
  starting transfers between devices: 81.7 us -> 0 us
  local copies, waits for them, and re-layouts: 77.3 us -> 1.28 us
  other arithmetic: 38.1 us -> 0 us
  matrix products: 17 us -> 0 us
    pallas_call x0 -> x3, Pallas kernels: none -> 180 us  [the longest x1 171 us: on_device(): pl.pallas_call(velocity_kernel, name='velocity', out_shape=(jax.ShapeDtyp...]
    psum x2 -> x0, blocking collectives: 167 us -> none  [on_device(): lax.psum((jnp.sum(direction * gradient), jnp.sum(curvature * direction *...]
    all_to_all x1 -> x0, waiting for transfers between devices: 114 us -> none  [on_device(): lax.all_to_all(jnp.stack([forward_rows, backward_rows]), 'slab', split_ax...]
    ppermute x18 -> x0, starting transfers between devices: 66.4 us -> none  [the longest x10 23.7 us: passed_along(): return lax.ppermute(block, axis, route)]
    gather x5 -> x0, local copies, waits for them, and re-layouts: 38 us -> none  [the longest x1 21.5 us: on_device(): fetched = arrived[direction_ids, peer_ids, slot_ids]]
    all_to_all x1 -> x0, blocking collectives: 23.1 us -> none  [on_device(): lax.all_to_all(request_table, 'slab', split_axis=1, concat_axis=1, tiled=...]
    dot_general x8 -> x0, matrix products: 17 us -> none  [prefilter(): jnp.dot(window, matrix, preferred_element_type=jnp.float32, precision=lax...]
    all_to_all x1 -> x0, starting transfers between devices: 15.3 us -> none  [on_device(): lax.all_to_all(jnp.stack([forward_rows, backward_rows]), 'slab', split_ax...]
  transfers between devices with their start and end apart: 19 -> 0, of which waited for: 4 -> 0; matrix products, arithmetic and copies ran while one was open for 16% -> 0% of each run, Pallas kernels for 0% -> 0%
where the time goes in v2:
time: 182 us
  Pallas kernels  180 us (99%)
    pallas_call x1, Pallas kernels, on_device(): pl.pallas_call(velocity_kernel, name='velocity', out_shape=(jax.ShapeDtyp...  171 us
    pallas_call x1, Pallas kernels, on_device(): pl.pallas_call(misfit_kernel, name='misfit', grid=(rows // block,), out_s...  6.87 us

profile of v2, /device:TPU:1, one launch (start us, length us, event | category | flops | bytes accessed | tf_op | source)
XLA Modules:
  0.0 182.0 jit_solution(10093751788296247162)
XLA Ops:
  0.6 1.3 copy.12
  1.9 2.2 %slots.1 = (s32[2,64,128]{2,1,0:T(8,128)}, s32[2,64,128]{2,1,0:T(8,128)}, s32[2,512]{1,0:T(2,128)}) custom-call(s32[2,512]{1,0:T(2,128)} %bitcast.9, s32[2,512]{1,0:T(2,128)} %bitcast.10), custom_call_target="tpu_custom_call" | custom-call | tf_op jit(solution)/shard_map/slots/pallas_call | solution.py:658
  4.2 171.0 %velocity.1 = (f32[1,512]{1,0:T(1,128)}, f32[512,8,128]{2,1,0:T(8,128)}, f32[512,8,128]{2,1,0:T(8,128)}, f32[512,8,128]{2,1,0:T(8,128)}) custom-call(f32[4]{0:T(128)} %table_ref.1, s32[2,64,128]{2,1,0:T(8,128)} %get-tuple-element.11.wanting_scalar, s32[2,512]{1,0:T(2,128)} %get-tuple-element.12.place_scalar.place, s32[2,64,1,128]{3,2,1,0:T(1,128)} %bitcast.8, ...), custom_call_target="tpu_custom_call" | custom-call | tf_op jit(solution)/shard_map/velocity/pallas_call | solution.py:670
  175.1 6.9 %misfit.1 = (f32[512,1024]{1,0:T(8,128)}, f32[1,512]{1,0:T(1,128)}) custom-call(f32[1,512]{1,0:T(1,128)} %get-tuple-element.14.velocity_ref, f32[512,8,128]{2,1,0:T(8,128)} %get-tuple-element.15.part0_ref, f32[512,8,128]{2,1,0:T(8,128)} %get-tuple-element.16.part1_ref, f32[512,8,128]{2,1,0:T(8,128)} %get-tuple-element.17.part2_ref), custom_call_target="tpu_custom_call" | custom-call | tf_op jit(solution)/shard_map/misfit/pallas_call | solution.py:718

commit v3 on v2

--- a/solution.py
+++ b/solution.py
@@ -15,7 +15,7 @@
 SCANS = 4
 SLABS = 64
 LAYERS = 8
-BATCH = 4
+BATCH = 2
 MESH = pl.DeviceIdType.MESH
 MIB = 1024 * 1024
 
@@ -36,18 +36,27 @@
     return jnp.asarray(np.concatenate([high, high])), jnp.asarray(low)
 
 
+def over(number, by):
+    return lax.div(number, jnp.int32(by))
+
+
+def left_of(number, by):
+    return lax.rem(number, jnp.int32(by))
+
+
 def shifts(number):
-    phase = number % 8
-    wave = number // 8
-    shift_z = jnp.where(phase % 2 == 0, (8 - phase // 2) % 8, (phase + 1) // 2)
-    return shift_z, 2 * (wave % 2) + wave // 4, (wave // 2) % 2
+    phase = left_of(number, 8)
+    wave = over(number, 8)
+    half = over(phase + 1, 2)
+    shift_z = jnp.where(left_of(phase, 2) == 0, left_of(8 - half, 8), half)
+    return shift_z, 2 * left_of(wave, 2) + over(wave, 4), left_of(over(wave, 2), 2)
 
 
 def displaced(slab, number):
     shift_z, shift_x, shift_c = shifts(number)
-    core = (slab % 2 + shift_c) % 2
-    at_x = ((slab // 2) % 4 + shift_x) % 4
-    at_z = (slab // 8 + shift_z) % 8
+    core = left_of(left_of(slab, 2) + shift_c, 2)
+    at_x = left_of(over(slab, 2) + shift_x, 4)
+    at_z = left_of(over(slab, 8) + shift_z, 8)
     return (at_z * 4 + at_x) * 2 + core
 
 
@@ -96,7 +105,7 @@
     out_ref, part0_ref, part1_ref, part2_ref,
     volume, by_row, asked, asked_scalar,
     packed, relay, arrived, value, slope, bend, middle, beside, own, sums, chosen, parts_buf,
-    near_box, far_box, totals,
+    turned, near_box, far_box, totals,
     volume_sem, ask_send, ask_recv, scalar_sem, row_send, row_recv, relay_recv, relay_send,
     near_send, near_recv, far_send, far_recv, part_sem,
 ):
@@ -120,11 +129,11 @@
     barrier = pltpu.get_barrier_semaphore()
 
     def near_peer(number):
-        return (scan, layer * group + (position + 1 + number) % group)
+        return (scan, layer * group + left_of(position + 1 + number, group))
 
     def far_peer(number):
-        other = (scan * LAYERS + layer + 1 + number) % fars
-        return (other // LAYERS, (other % LAYERS) * group + position)
+        other = left_of(scan * LAYERS + layer + 1 + number, fars)
+        return (over(other, LAYERS), left_of(other, LAYERS) * group + position)
 
     below = jnp.logical_and(layer >= 1, position <= 1)
     above = layer <= LAYERS - 2
@@ -196,7 +205,7 @@
         )
 
     def ask(number, carry):
-        target = displaced(slab, number)
+        target = left_of(slab + number, SLABS)
 
         @pl.when(up)
         def _():
@@ -290,22 +299,20 @@
         weight = jnp.where(class_ref[...] == number, table_ref[number], weight)
     stiffness = jnp.sqrt(weight)
     velocity = velocity_ref[...]
-    blank = jnp.zeros((1, 2 * LANES), jnp.float32)
-    share(0, jnp.concatenate([stiffness * velocity, blank], axis=1))
-
-    def take_asked(side):
-        whole_ask(side).wait_recv()
-        copy = pltpu.make_async_copy(asked.at[side], asked_scalar.at[side], scalar_sem)
-        copy.start()
-        copy.wait()
-
-    @pl.when(down)
-    def _():
-        take_asked(0)
-
-    @pl.when(up)
-    def _():
-        take_asked(1)
+
+    def scalar_copy(side):
+        return pltpu.make_async_copy(asked.at[side], asked_scalar.at[side], scalar_sem.at[side])
+
+    for side, serving in ((0, down), (1, up)):
+        @pl.when(serving)
+        def _():
+            whole_ask(side).wait_recv()
+            scalar_copy(side).start()
+
+    for side, serving in ((0, down), (1, up)):
+        @pl.when(serving)
+        def _():
+            scalar_copy(side).wait()
 
     def row_copy(source, side, number, target, target_scan, send_sem):
         return pltpu.make_async_remote_copy(
@@ -358,6 +365,8 @@
         return carry
 
     lax.fori_loop(0, SLABS, send, 0)
+    blank = jnp.zeros((1, 2 * LANES), jnp.float32)
+    share(0, jnp.concatenate([stiffness * velocity, blank], axis=1))
 
     for side in range(2):
         across = place[side : side + 1, :].astype(jnp.float32)
@@ -372,9 +381,6 @@
         @pl.when(jnp.logical_not(present[side]))
         def _():
             sums[side] = jnp.zeros(sums.shape[1:], jnp.float32)
-
-    collect(0)
-    smooth = stencil(0, stiffness * velocity)
 
     lane8 = lax.broadcasted_iota(jnp.int32, (8, LANES), 1)
     zero8 = jnp.zeros((8, LANES), jnp.float32)
@@ -445,9 +451,9 @@
 
     def displaced_back(number):
         shift_z, shift_x, shift_c = shifts(number)
-        core = (slab % 2 + 2 - shift_c) % 2
-        at_x = ((slab // 2) % 4 + 4 - shift_x) % 4
-        at_z = (slab // 8 + 8 - shift_z) % 8
+        core = left_of(left_of(slab, 2) + 2 - shift_c, 2)
+        at_x = left_of(over(slab, 2) + 4 - shift_x, 4)
+        at_z = left_of(over(slab, 8) + 8 - shift_z, 8)
         return (at_z * 4 + at_x) * 2 + core
 
     def pass_on(side, relay_number):
@@ -473,6 +479,8 @@
 
     lax.fori_loop(0, SLABS // BATCH, step, 0)
 
+    collect(0)
+    smooth = stencil(0, stiffness * velocity)
     moments = jnp.dot(
         chosen[...],
         sums[...].reshape(2 * SLABS * CAP, LANES).astype(jnp.bfloat16),
@@ -483,7 +491,7 @@
     m0, m1, m2, m3, m4 = (moments[number : number + 1, :] for number in range(5))
 
     def coefficients(quarter):
-        def one_row(row):
+        def one_row(row, at):
             forward = place_scalar[0, row]
             backward = place_scalar[1, row]
 
@@ -496,16 +504,23 @@
             value_f, value_b = got(value)
             slope_f, slope_b = got(slope)
             bend_f, bend_b = got(bend)
-            parts_buf[0, row] = value_f + value_b - 2.0 * by_row[row]
-            parts_buf[1, row] = slope_f - slope_b
-            parts_buf[2, row] = 0.5 * (bend_f + bend_b)
-
-        def four(step, carry):
-            for one in range(4):
-                one_row(quarter * (rows // 4) + step * 4 + one)
+            turned[0, at] = value_f + value_b - 2.0 * by_row[row]
+            turned[1, at] = slope_f - slope_b
+            turned[2, at] = 0.5 * (bend_f + bend_b)
+
+        def eight(step, carry):
+            base = pl.multiple_of(quarter * (rows // 4) + step * 8, 8)
+            half = (step % 2) * 8
+            for one in range(8):
+                one_row(base + one, half + one)
+            for number in range(3):
+                for block in range(blocks):
+                    parts_buf[number, pl.ds(base, 8), block * LANES : (block + 1) * LANES] = turned[
+                        number, pl.ds(pl.multiple_of(half, 8), 8), block, :
+                    ]
             return carry
 
-        lax.fori_loop(0, rows // 16, four, 0)
+        lax.fori_loop(0, rows // 32, eight, 0)
         for copy in part_copies(quarter):
             copy.start()
 
@@ -623,22 +638,16 @@
             copy.wait()
 
 
-def misfit_kernel(velocity_ref, part0_ref, part1_ref, part2_ref, out_ref, velocity_out_ref, upright):
+def misfit_kernel(velocity_ref, part0_ref, part1_ref, part2_ref, out_ref, velocity_out_ref):
     rows = out_ref.shape[0]
     across = velocity_ref[...]
     velocity_out_ref[...] = across
-    upright[...] = jnp.transpose(jnp.broadcast_to(across, (rows, rows)))
-
-    def eight(step, carry):
-        at = pl.ds(pl.multiple_of(step * 8, 8), 8)
-        moved = upright[at, :]
-        for block in range(out_ref.shape[1] // LANES):
-            out_ref[at, block * LANES : (block + 1) * LANES] = part0_ref[at, block, :] + moved * (
-                part1_ref[at, block, :] + moved * part2_ref[at, block, :]
-            )
-        return carry
-
-    lax.fori_loop(0, rows // 8, eight, 0, unroll=2)
+    moved = jnp.transpose(jnp.broadcast_to(across, (rows, rows)))
+    for at in range(0, out_ref.shape[1], LANES):
+        columns = slice(at, at + LANES)
+        out_ref[:, columns] = part0_ref[:, columns] + moved * (
+            part1_ref[:, columns] + moved * part2_ref[:, columns]
+        )
 
 
 def on_device(volume, velocity0, fetch_slab, fetch_row, modulus_class, modulus_table):
@@ -672,9 +681,9 @@
         name="velocity",
         out_shape=(
             jax.ShapeDtypeStruct((1, rows), f32),
-            jax.ShapeDtypeStruct((rows,) + tile, f32),
-            jax.ShapeDtypeStruct((rows,) + tile, f32),
-            jax.ShapeDtypeStruct((rows,) + tile, f32),
+            jax.ShapeDtypeStruct((rows, length), f32),
+            jax.ShapeDtypeStruct((rows, length), f32),
+            jax.ShapeDtypeStruct((rows, length), f32),
         ),
         in_specs=[smem, smem, smem, vmem, vmem, anywhere, vmem, vmem, vmem, vmem],
         out_specs=(vmem, anywhere, anywhere, anywhere),
@@ -694,11 +703,12 @@
             pltpu.VMEM((BATCH * CAP,) + tile, f32),
             pltpu.VMEM((2, SLABS * CAP, LANES), f32),
             pltpu.VMEM((rows, 2 * SLABS * CAP), jnp.bfloat16),
-            pltpu.VMEM((3, rows) + tile, f32),
+            pltpu.VMEM((3, rows, length), f32),
+            pltpu.VMEM((3, 16) + tile, f32),
             pltpu.VMEM((turns, 12, 1, wide), f32),
             pltpu.VMEM((ITERS, SCANS * LAYERS - 1, 1, 2 * LANES), f32),
             pltpu.VMEM((ITERS, 1, 2 * LANES), f32),
-            dma, dma((2,)), dma((2,)), dma, dma((2,)), dma((2, SLABS)),
+            dma, dma((2,)), dma((2,)), dma((2,)), dma((2,)), dma((2, SLABS)),
             dma((SLABS // 2,)), dma,
             dma((turns, 15)), dma((turns, 12)),
             dma((ITERS, SCANS * LAYERS - 1)), dma((ITERS, SCANS * LAYERS - 1)),
@@ -714,7 +724,7 @@
 
     block = 128
     across = pl.BlockSpec((1, block), lambda step: (0, step))
-    tiles = pl.BlockSpec((block,) + tile, lambda step: (step, 0, 0))
+    wide_rows = pl.BlockSpec((block, length), lambda step: (step, 0))
     misfit, velocity = pl.pallas_call(
         misfit_kernel,
         name="misfit",
@@ -723,9 +733,8 @@
             jax.ShapeDtypeStruct((rows, length), f32),
             jax.ShapeDtypeStruct((1, rows), f32),
         ),
-        in_specs=[across, tiles, tiles, tiles],
-        out_specs=(pl.BlockSpec((block, length), lambda step: (step, 0)), across),
-        scratch_shapes=[pltpu.VMEM((block, block), f32)],
+        in_specs=[across, wide_rows, wide_rows, wide_rows],
+        out_specs=(wide_rows, across),
     )(velocity, part0, part1, part2)
     return velocity, misfit.reshape(volume.shape)
 

time: 182 us -> 177 us (0.973)
  Pallas kernels: 180 us -> 175 us
    pallas_call x1, Pallas kernels: 171 us -> 168 us  [on_device(): pl.pallas_call(velocity_kernel, name='velocity', out_shape=(jax.ShapeDtyp...]
    pallas_call x1, Pallas kernels: 6.87 us -> 4.78 us  [on_device(): pl.pallas_call(misfit_kernel, name='misfit', grid=(rows // block,), out_s...]
where the time goes in v3:
time: 177 us
  Pallas kernels  175 us (99%)
    pallas_call x1, Pallas kernels, on_device(): pl.pallas_call(velocity_kernel, name='velocity', out_shape=(jax.ShapeDtyp...  168 us
    pallas_call x1, Pallas kernels, on_device(): pl.pallas_call(misfit_kernel, name='misfit', grid=(rows // block,), out_s...  4.78 us

profile of v3, /device:TPU:1, one launch (start us, length us, event | category | flops | bytes accessed | tf_op | source)
XLA Modules:
  0.0 176.5 jit_solution(15552767381582941469)
XLA Ops:
  0.6 1.3 copy.12
  1.9 2.2 %slots.1 = (s32[2,64,128]{2,1,0:T(8,128)}, s32[2,64,128]{2,1,0:T(8,128)}, s32[2,512]{1,0:T(2,128)}) custom-call(s32[2,512]{1,0:T(2,128)} %bitcast.9, s32[2,512]{1,0:T(2,128)} %bitcast.10), custom_call_target="tpu_custom_call" | custom-call | tf_op jit(solution)/shard_map/slots/pallas_call | solution.py:667
  4.2 167.6 %velocity.1 = (f32[1,512]{1,0:T(1,128)}, f32[512,1024]{1,0:T(8,128)}, f32[512,1024]{1,0:T(8,128)}, f32[512,1024]{1,0:T(8,128)}) custom-call(f32[4]{0:T(128)} %table_ref.1, s32[2,64,128]{2,1,0:T(8,128)} %get-tuple-element.11.wanting_scalar, s32[2,512]{1,0:T(2,128)} %get-tuple-element.12.place_scalar.place, s32[2,64,1,128]{3,2,1,0:T(1,128)} %bitcast.8, ...), custom_call_target="tpu_custom_call" | custom-call | tf_op jit(solution)/shard_map/velocity/pallas_call | solution.py:679
  171.7 4.8 %misfit.1 = (f32[512,1024]{1,0:T(8,128)}, f32[1,512]{1,0:T(1,128)}) custom-call(f32[1,512]{1,0:T(1,128)} %get-tuple-element.14.velocity_ref, f32[512,1024]{1,0:T(8,128)} %get-tuple-element.15.part0_ref, f32[512,1024]{1,0:T(8,128)} %get-tuple-element.16.part1_ref, f32[512,1024]{1,0:T(8,128)} %get-tuple-element.17.part2_ref), custom_call_target="tpu_custom_call" | custom-call | tf_op jit(solution)/shard_map/misfit/pallas_call | solution.py:728

commit v4 on v3

--- a/solution.py
+++ b/solution.py
@@ -69,41 +69,10 @@
     return wave * 8 + phase
 
 
-def slots_kernel(peer_ref, row_ref, request_ref, wanting_ref, place_ref):
-    slab = lax.axis_index("slab")
-    rows = peer_ref.shape[1]
-    earlier = (
-        lax.broadcasted_iota(jnp.int32, (rows, rows), 0)
-        < lax.broadcasted_iota(jnp.int32, (rows, rows), 1)
-    ).astype(jnp.float32).astype(jnp.bfloat16)
-    contract = (((1,), (1,)), ((), ()))
-    here = lax.broadcasted_iota(jnp.int32, (1, rows), 1)
-    for side in range(2):
-        peer = peer_ref[side : side + 1, :]
-        named = (lax.broadcasted_iota(jnp.int32, (SLABS, rows), 0) == peer).astype(jnp.float32)
-        named16 = named.astype(jnp.bfloat16)
-        before = jnp.dot(named16, earlier, preferred_element_type=jnp.float32)
-        slot = jnp.sum(before * named, axis=0, keepdims=True).astype(jnp.int32)
-        at_slot = (lax.broadcasted_iota(jnp.int32, (LANES, rows), 0) == slot).astype(jnp.float32)
-
-        def tabled(numbers):
-            high = (at_slot * (numbers // 16).astype(jnp.float32)).astype(jnp.bfloat16)
-            low = (at_slot * (numbers % 16).astype(jnp.float32)).astype(jnp.bfloat16)
-            return (
-                16.0 * lax.dot_general(named16, high, contract, preferred_element_type=jnp.float32)
-                + lax.dot_general(named16, low, contract, preferred_element_type=jnp.float32)
-            ).astype(jnp.int32)
-
-        request_ref[side] = tabled(row_ref[side : side + 1, :])
-        wanting_ref[side] = tabled(here)
-        place_ref[side : side + 1, :] = number_between(peer, slab) * CAP + jnp.minimum(slot, CAP - 1)
-
-
 def velocity_kernel(
-    table_ref, wanting_scalar, place_scalar, request, place, volume_ref, velocity_ref, class_ref,
-    high_ref, low_ref,
+    table_ref, peer_ref, row_ref, volume_ref, velocity_ref, class_ref, high_ref, low_ref,
     out_ref, part0_ref, part1_ref, part2_ref,
-    volume, by_row, asked, asked_scalar,
+    volume, by_row, request, wanting, place, asked, asked_scalar, wanting_scalar, place_scalar,
     packed, relay, arrived, value, slope, bend, middle, beside, own, sums, chosen, parts_buf,
     turned, near_box, far_box, totals,
     volume_sem, ask_send, ask_recv, scalar_sem, row_send, row_recv, relay_recv, relay_send,
@@ -181,6 +150,34 @@
         + jnp.where(above, 2, 0) + jnp.where(below, group, 0)
     )
 
+    earlier = (
+        lax.broadcasted_iota(jnp.int32, (rows, rows), 0)
+        < lax.broadcasted_iota(jnp.int32, (rows, rows), 1)
+    ).astype(jnp.float32).astype(jnp.bfloat16)
+    contract = (((1,), (1,)), ((), ()))
+    here = lax.broadcasted_iota(jnp.int32, (1, rows), 1)
+    for side in range(2):
+        peer = peer_ref[side : side + 1, :]
+        named = (lax.broadcasted_iota(jnp.int32, (SLABS, rows), 0) == peer).astype(jnp.float32)
+        named16 = named.astype(jnp.bfloat16)
+        before = jnp.dot(named16, earlier, preferred_element_type=jnp.float32)
+        slot = jnp.sum(before * named, axis=0, keepdims=True).astype(jnp.int32)
+        at_slot = (lax.broadcasted_iota(jnp.int32, (LANES, rows), 0) == slot).astype(jnp.float32)
+
+        def tabled(numbers):
+            high = (at_slot * (numbers // 16).astype(jnp.float32)).astype(jnp.bfloat16)
+            low = (at_slot * (numbers % 16).astype(jnp.float32)).astype(jnp.bfloat16)
+            table = (
+                16.0 * lax.dot_general(named16, high, contract, preferred_element_type=jnp.float32)
+                + lax.dot_general(named16, low, contract, preferred_element_type=jnp.float32)
+            ).astype(jnp.int32)
+            return jnp.clip(table, 0, rows - 1)
+
+        request[side, :, 0, :] = tabled(row_ref[side : side + 1, :])
+        wanting[side, :, 0, :] = tabled(here)
+        at = number_between(peer, slab) * CAP + jnp.clip(slot, 0, CAP - 1)
+        place[side : side + 1, :] = jnp.clip(at, 0, SLABS * CAP - 1)
+
     volume_copy.wait()
 
     def relayout(block, carry):
@@ -300,6 +297,11 @@
     stiffness = jnp.sqrt(weight)
     velocity = velocity_ref[...]
 
+    wanting_copy = pltpu.make_async_copy(wanting, wanting_scalar, scalar_sem.at[2])
+    place_copy = pltpu.make_async_copy(place, place_scalar, scalar_sem.at[3])
+    wanting_copy.start()
+    place_copy.start()
+
     def scalar_copy(side):
         return pltpu.make_async_copy(asked.at[side], asked_scalar.at[side], scalar_sem.at[side])
 
@@ -368,6 +370,8 @@
     blank = jnp.zeros((1, 2 * LANES), jnp.float32)
     share(0, jnp.concatenate([stiffness * velocity, blank], axis=1))
 
+    wanting_copy.wait()
+    place_copy.wait()
     for side in range(2):
         across = place[side : side + 1, :].astype(jnp.float32)
         upright = jnp.transpose(jnp.broadcast_to(across, (LANES, rows)))
@@ -401,7 +405,7 @@
         for chunk in range(BATCH):
             source = displaced_back(batch * BATCH + chunk)
             for slot in range(CAP):
-                own[chunk * CAP + slot] = by_row[wanting_scalar[side, source, slot]]
+                own[chunk * CAP + slot] = by_row[wanting_scalar[side, source, 0, slot]]
 
         def combine(eight, carry):
             at = pl.ds(pl.multiple_of(eight * 8, 8), 8)
@@ -664,18 +668,6 @@
     turns = ITERS + 1
     wide = rows + 2 * LANES
 
-    request, wanting, place = pl.pallas_call(
-        slots_kernel,
-        name="slots",
-        out_shape=(
-            jax.ShapeDtypeStruct((2, SLABS, LANES), i32),
-            jax.ShapeDtypeStruct((2, SLABS, LANES), i32),
-            jax.ShapeDtypeStruct((2, rows), i32),
-        ),
-        in_specs=[vmem, vmem],
-        out_specs=(vmem, vmem, vmem),
-    )(fetch_slab.reshape(2, rows), fetch_row.reshape(2, rows))
-
     velocity, part0, part1, part2 = pl.pallas_call(
         velocity_kernel,
         name="velocity",
@@ -685,13 +677,18 @@
             jax.ShapeDtypeStruct((rows, length), f32),
             jax.ShapeDtypeStruct((rows, length), f32),
         ),
-        in_specs=[smem, smem, smem, vmem, vmem, anywhere, vmem, vmem, vmem, vmem],
+        in_specs=[smem, vmem, vmem, anywhere, vmem, vmem, vmem, vmem],
         out_specs=(vmem, anywhere, anywhere, anywhere),
         scratch_shapes=[
             pltpu.VMEM((rows, length), f32),
             pltpu.VMEM((rows,) + tile, f32),
             pltpu.VMEM((2, SLABS, 1, LANES), i32),
+            pltpu.VMEM((2, SLABS, 1, LANES), i32),
+            pltpu.VMEM((2, rows), i32),
+            pltpu.VMEM((2, SLABS, 1, LANES), i32),
             pltpu.SMEM((2, SLABS, 1, LANES), i32),
+            pltpu.SMEM((2, SLABS, 1, LANES), i32),
+            pltpu.SMEM((2, rows), i32),
             pltpu.VMEM((2, SLABS, CAP) + tile, f32),
             pltpu.VMEM((SLABS // 2, CAP) + tile, f32),
             pltpu.VMEM((2, SLABS, CAP) + tile, f32),
@@ -708,7 +705,7 @@
             pltpu.VMEM((turns, 12, 1, wide), f32),
             pltpu.VMEM((ITERS, SCANS * LAYERS - 1, 1, 2 * LANES), f32),
             pltpu.VMEM((ITERS, 1, 2 * LANES), f32),
-            dma, dma((2,)), dma((2,)), dma((2,)), dma((2,)), dma((2, SLABS)),
+            dma, dma((2,)), dma((2,)), dma((4,)), dma((2,)), dma((2, SLABS)),
             dma((SLABS // 2,)), dma,
             dma((turns, 15)), dma((turns, 12)),
             dma((ITERS, SCANS * LAYERS - 1)), dma((ITERS, SCANS * LAYERS - 1)),
@@ -718,7 +715,7 @@
             collective_id=0, has_side_effects=True, vmem_limit_bytes=56 * MIB
         ),
     )(
-        modulus_table, wanting, place, request.reshape(2, SLABS, 1, LANES), place,
+        modulus_table, fetch_slab.reshape(2, rows), fetch_row.reshape(2, rows),
         volume.reshape(rows, length), velocity0, modulus_class, high, low,
     )
 

time: 177 us -> 176 us (level)
    pallas_call x1 -> x0, Pallas kernels: 2.24 us -> none  [on_device(): pl.pallas_call(slots_kernel, name='slots', out_shape=(jax.ShapeDtypeStruc...]
    pallas_call x1, Pallas kernels: 168 us -> 170 us  [on_device(): pl.pallas_call(velocity_kernel, name='velocity', out_shape=(jax.ShapeDtyp...]
where the time goes in v4:
time: 176 us
  Pallas kernels  174 us (99%)
    pallas_call x1, Pallas kernels, on_device(): pl.pallas_call(velocity_kernel, name='velocity', out_shape=(jax.ShapeDtyp...  170 us
    pallas_call x1, Pallas kernels, on_device(): pl.pallas_call(misfit_kernel, name='misfit', grid=(rows // block,), out_s...  4.78 us

profile of v4, /device:TPU:1, one launch (start us, length us, event | category | flops | bytes accessed | tf_op | source)
XLA Modules:
  0.0 176.2 jit_solution(11670543415554603735)
XLA Ops:
  0.6 1.3 copy.12
  1.9 169.5 %velocity.1 = (f32[1,512]{1,0:T(1,128)}, f32[512,1024]{1,0:T(8,128)}, f32[512,1024]{1,0:T(8,128)}, f32[512,1024]{1,0:T(8,128)}) custom-call(f32[4]{0:T(128)} %table_ref.1, s32[2,512]{1,0:T(2,128)} %bitcast.7, s32[2,512]{1,0:T(2,128)} %bitcast.8, f32[512,1024]{1,0:T(8,128)} %bitcast.6, f32[1,512]{1,0:T(1,128)} %velocity_ref.1, s32[1,512]{1,0:T(1,128)} %class_ref.1, ...), custom_call_target="tpu_custom_call" | custom-call | tf_op jit(solution)/shard_map/velocity/pallas_call | solution.py:671
  171.4 4.8 %misfit.1 = (f32[512,1024]{1,0:T(8,128)}, f32[1,512]{1,0:T(1,128)}) custom-call(f32[1,512]{1,0:T(1,128)} %get-tuple-element.8.velocity_ref, f32[512,1024]{1,0:T(8,128)} %get-tuple-element.9.part0_ref, f32[512,1024]{1,0:T(8,128)} %get-tuple-element.10.part1_ref, f32[512,1024]{1,0:T(8,128)} %get-tuple-element.11.part2_ref), custom_call_target="tpu_custom_call" | custom-call | tf_op jit(solution)/shard_map/misfit/pallas_call | solution.py:725

commit v5 on v4

--- a/solution.py
+++ b/solution.py
@@ -120,35 +120,10 @@
         def _():
             greet((scan + 1, number))
 
-        @pl.when(jnp.logical_and(edge, number != slab))
-        def _():
-            greet((scan, number))
-
         return carry
 
-    def greet_far(number, carry):
-        greet(far_peer(number))
-        return carry
-
     lax.fori_loop(0, SLABS, greet_rows, 0)
-    lax.fori_loop(0, fars - 1, greet_far, 0)
-    for number in range(group - 1):
-        greet(near_peer(number))
-
-    @pl.when(above)
-    def _():
-        for number in range(2):
-            greet((scan, (layer + 1) * group + number))
-
-    @pl.when(below)
-    def _():
-        for number in range(group):
-            greet((scan, (layer - 1) * group + number))
-
-    expected = (
-        jnp.where(edge, 2 * SLABS - 1, 2 * SLABS) + fars - 1 + group - 1
-        + jnp.where(above, 2, 0) + jnp.where(below, group, 0)
-    )
+    expected = jnp.where(edge, SLABS, 2 * SLABS)
 
     earlier = (
         lax.broadcasted_iota(jnp.int32, (rows, rows), 0)
@@ -272,8 +247,6 @@
         def _():
             wait(0)
             wait(1)
-
-        shares(turn, lambda copy: copy.wait_send())
 
     lane_row = lax.broadcasted_iota(jnp.int32, (1, rows), 1)
 
@@ -481,15 +454,26 @@
 
         return carry
 
-    lax.fori_loop(0, SLABS // BATCH, step, 0)
+    def moments_of(first, count):
+        at = slice(first, first + count)
+        return sum(
+            jnp.dot(
+                chosen[:, side * SLABS * CAP + first : side * SLABS * CAP + first + count],
+                sums[side, at, :].astype(jnp.bfloat16),
+                preferred_element_type=jnp.float32,
+            )
+            for side in range(2)
+        )
+
+    settled = 512
+    steps = SLABS // BATCH
+    lax.fori_loop(0, 3 * steps // 4, step, 0)
+    moments = moments_of(0, settled)
+    lax.fori_loop(3 * steps // 4, steps, step, 0)
 
     collect(0)
     smooth = stencil(0, stiffness * velocity)
-    moments = jnp.dot(
-        chosen[...],
-        sums[...].reshape(2 * SLABS * CAP, LANES).astype(jnp.bfloat16),
-        preferred_element_type=jnp.float32,
-    )
+    moments = moments + moments_of(settled, SLABS * CAP - settled)
     moments = jnp.transpose(moments)
     moments = moments[0:8] + moments[8:16] + moments[16:24]
     m0, m1, m2, m3, m4 = (moments[number : number + 1, :] for number in range(5))
@@ -537,6 +521,16 @@
 
     def folded(values):
         return sum(values[:, at : at + LANES] for at in range(0, rows, LANES))
+
+    def far_copy(turn, number):
+        return pltpu.make_async_remote_copy(
+            src_ref=totals.at[turn],
+            dst_ref=far_box.at[turn, number],
+            send_sem=far_send.at[turn, number],
+            recv_sem=far_recv.at[turn, number],
+            device_id=far_peer(number),
+            device_id_type=MESH,
+        )
 
     for turn in range(ITERS):
         linear = m0 + velocity * (m1 + m2) + 1.5 * velocity * velocity * m3 + (
@@ -576,22 +570,12 @@
         mine = mine - jnp.concatenate([jnp.zeros_like(cross), 2.0 * cross], axis=1)
         totals[turn] = mine
 
-        def far_copy(number):
-            return pltpu.make_async_remote_copy(
-                src_ref=totals.at[turn],
-                dst_ref=far_box.at[turn, number],
-                send_sem=far_send.at[turn, number],
-                recv_sem=far_recv.at[turn, number],
-                device_id=far_peer(number),
-                device_id_type=MESH,
-            )
-
         def far_start(number, carry):
-            far_copy(number).start()
+            far_copy(turn, number).start()
             return carry
 
         def far_wait(number, carry):
-            far_copy(number).wait()
+            far_copy(turn, number).wait_recv()
             return carry
 
         lax.fori_loop(0, fars - 1, far_start, 0)
@@ -605,6 +589,16 @@
         velocity = velocity - alpha * direction
         smooth = smooth - alpha * bent
     out_ref[...] = velocity
+
+    for turn in range(ITERS + 1):
+        shares(turn, lambda copy: copy.wait_send())
+
+    def far_left(number, carry):
+        for turn in range(ITERS):
+            far_copy(turn, number).wait_send()
+        return carry
+
+    lax.fori_loop(0, fars - 1, far_left, 0)
 
     @pl.when(up)
     def _():

time: 176 us -> 173 us (0.983)
  Pallas kernels: 174 us -> 171 us
    pallas_call x1, Pallas kernels: 170 us -> 166 us  [on_device(): pl.pallas_call(velocity_kernel, name='velocity', out_shape=(jax.ShapeDtyp...]
where the time goes in v5:
time: 173 us
  Pallas kernels  171 us (99%)
    pallas_call x1, Pallas kernels, on_device(): pl.pallas_call(velocity_kernel, name='velocity', out_shape=(jax.ShapeDtyp...  166 us
    pallas_call x1, Pallas kernels, on_device(): pl.pallas_call(misfit_kernel, name='misfit', grid=(rows // block,), out_s...  4.78 us

profile of v5, /device:TPU:1, one launch (start us, length us, event | category | flops | bytes accessed | tf_op | source)
XLA Modules:
  0.0 172.6 jit_solution(17690442341190034446)
XLA Ops:
  0.6 1.3 copy.12
  1.9 165.9 %velocity.1 = (f32[1,512]{1,0:T(1,128)}, f32[512,1024]{1,0:T(8,128)}, f32[512,1024]{1,0:T(8,128)}, f32[512,1024]{1,0:T(8,128)}) custom-call(f32[4]{0:T(128)} %table_ref.1, s32[2,512]{1,0:T(2,128)} %bitcast.7, s32[2,512]{1,0:T(2,128)} %bitcast.8, f32[512,1024]{1,0:T(8,128)} %bitcast.6, f32[1,512]{1,0:T(1,128)} %velocity_ref.1, s32[1,512]{1,0:T(1,128)} %class_ref.1, ...), custom_call_target="tpu_custom_call" | custom-call | tf_op jit(solution)/shard_map/velocity/pallas_call | solution.py:665
  167.8 4.8 %misfit.1 = (f32[512,1024]{1,0:T(8,128)}, f32[1,512]{1,0:T(1,128)}) custom-call(f32[1,512]{1,0:T(1,128)} %get-tuple-element.8.velocity_ref, f32[512,1024]{1,0:T(8,128)} %get-tuple-element.9.part0_ref, f32[512,1024]{1,0:T(8,128)} %get-tuple-element.10.part1_ref, f32[512,1024]{1,0:T(8,128)} %get-tuple-element.11.part2_ref), custom_call_target="tpu_custom_call" | custom-call | tf_op jit(solution)/shard_map/misfit/pallas_call | solution.py:719

commit v6 on v5

--- a/solution.py
+++ b/solution.py
@@ -532,6 +532,45 @@
             device_id_type=MESH,
         )
 
+    def rows_left():
+        @pl.when(up)
+        def _():
+            whole_ask(0).wait_send()
+
+        @pl.when(down)
+        def _():
+            whole_ask(1).wait_send()
+
+        for side, serving in ((0, down), (1, up)):
+            @pl.when(serving)
+            def _():
+                pltpu.make_async_remote_copy(
+                    src_ref=packed.at[side],
+                    dst_ref=arrived.at[side],
+                    send_sem=row_send.at[side],
+                    recv_sem=row_recv.at[side, 0],
+                    device_id=(scan, slab),
+                    device_id_type=MESH,
+                ).wait_send()
+
+        @pl.when(edge)
+        def _():
+            pltpu.make_async_remote_copy(
+                src_ref=relay,
+                dst_ref=relay,
+                send_sem=relay_send,
+                recv_sem=relay_recv.at[0],
+                device_id=(scan, slab),
+                device_id_type=MESH,
+            ).wait_send()
+
+    def far_left(turn):
+        def one(number, carry):
+            far_copy(turn, number).wait_send()
+            return carry
+
+        lax.fori_loop(0, fars - 1, one, 0)
+
     for turn in range(ITERS):
         linear = m0 + velocity * (m1 + m2) + 1.5 * velocity * velocity * m3 + (
             0.5 * velocity * velocity * velocity * m4
@@ -581,6 +620,12 @@
         lax.fori_loop(0, fars - 1, far_start, 0)
         bent = stencil(turn + 1, scaled)
         coefficients(2 * turn + 1)
+        shares(turn + 1, lambda copy: copy.wait_send())
+        if turn == 0:
+            rows_left()
+            shares(0, lambda copy: copy.wait_send())
+        else:
+            far_left(turn - 1)
         lax.fori_loop(0, fars - 1, far_wait, 0)
         mine = mine + jnp.sum(far_box[turn], axis=0)
         upper = jnp.sum(mine[:, :LANES], axis=1, keepdims=True)
@@ -590,47 +635,7 @@
         smooth = smooth - alpha * bent
     out_ref[...] = velocity
 
-    for turn in range(ITERS + 1):
-        shares(turn, lambda copy: copy.wait_send())
-
-    def far_left(number, carry):
-        for turn in range(ITERS):
-            far_copy(turn, number).wait_send()
-        return carry
-
-    lax.fori_loop(0, fars - 1, far_left, 0)
-
-    @pl.when(up)
-    def _():
-        whole_ask(0).wait_send()
-
-    @pl.when(down)
-    def _():
-        whole_ask(1).wait_send()
-
-    for side, serving in ((0, down), (1, up)):
-        @pl.when(serving)
-        def _():
-            pltpu.make_async_remote_copy(
-                src_ref=packed.at[side],
-                dst_ref=arrived.at[side],
-                send_sem=row_send.at[side],
-                recv_sem=row_recv.at[side, 0],
-                device_id=(scan, slab),
-                device_id_type=MESH,
-            ).wait_send()
-
-    @pl.when(edge)
-    def _():
-        pltpu.make_async_remote_copy(
-            src_ref=relay,
-            dst_ref=relay,
-            send_sem=relay_send,
-            recv_sem=relay_recv.at[0],
-            device_id=(scan, slab),
-            device_id_type=MESH,
-        ).wait_send()
-
+    far_left(ITERS - 1)
     for quarter in range(4):
         for copy in part_copies(quarter):
             copy.wait()

time: 173 us -> 173 us (level)
  no operation moved by 1% of the time
where the time goes in v6:
time: 173 us; the launch traced here: 172 us
  Pallas kernels  171 us (99%)
    pallas_call x1, Pallas kernels, on_device(): pl.pallas_call(velocity_kernel, name='velocity', out_shape=(jax.ShapeDtyp...  166 us
    pallas_call x1, Pallas kernels, on_device(): pl.pallas_call(misfit_kernel, name='misfit', grid=(rows // block,), out_s...  4.78 us

profile of v6, /device:TPU:1, one launch (start us, length us, event | category | flops | bytes accessed | tf_op | source)
XLA Modules:
  0.0 172.4 jit_solution(9688014901463312425)
XLA Ops:
  0.6 1.3 copy.12
  1.9 165.7 %velocity.1 = (f32[1,512]{1,0:T(1,128)}, f32[512,1024]{1,0:T(8,128)}, f32[512,1024]{1,0:T(8,128)}, f32[512,1024]{1,0:T(8,128)}) custom-call(f32[4]{0:T(128)} %table_ref.1, s32[2,512]{1,0:T(2,128)} %bitcast.7, s32[2,512]{1,0:T(2,128)} %bitcast.8, f32[512,1024]{1,0:T(8,128)} %bitcast.6, f32[1,512]{1,0:T(1,128)} %velocity_ref.1, s32[1,512]{1,0:T(1,128)} %class_ref.1, ...), custom_call_target="tpu_custom_call" | custom-call | tf_op jit(solution)/shard_map/velocity/pallas_call | solution.py:670
  167.6 4.8 %misfit.1 = (f32[512,1024]{1,0:T(8,128)}, f32[1,512]{1,0:T(1,128)}) custom-call(f32[1,512]{1,0:T(1,128)} %get-tuple-element.8.velocity_ref, f32[512,1024]{1,0:T(8,128)} %get-tuple-element.9.part0_ref, f32[512,1024]{1,0:T(8,128)} %get-tuple-element.10.part1_ref, f32[512,1024]{1,0:T(8,128)} %get-tuple-element.11.part2_ref), custom_call_target="tpu_custom_call" | custom-call | tf_op jit(solution)/shard_map/misfit/pallas_call | solution.py:724
